TPU v7x, 256 devices: a whole 4x4x8 slice. The times are simulated.
256 devices in a mesh: rep: 2 (over core), src: 16 (over z_lo, x), tgt: 8 (over z_hi, y).
Axes of the slice: x: 4, y: 4, z: 8 (z_hi: 2, z_lo: 4; z = z_hi * 4 + z_lo), core: 2. Of those that a mesh axis runs over, the one named last changes fastest.
Arguments:
- src_feats: float32 [2, 2048, 3200], P('rep', ('src', 'tgt')), may hold values from -6 to 6
- tgt_cotangent: float32 [2, 2048, 3200], P('rep', ('tgt', 'src')), may hold values from -0.6 to 0.6
- rotation: float32 [2, 16, 8, 115, 384], P('rep', 'src', 'tgt'), may hold values from -3 to 3
- edge_src: int32 [2, 16, 8, 384], P('rep', 'src', 'tgt'), may hold values from 0 to 127
- edge_tgt: int32 [2, 16, 8, 384], P('rep', 'src', 'tgt'), may hold values from 0 to 255
- edge_count: int32 [2, 16, 8], P('rep', 'src', 'tgt'), may hold values from 192 to 384, as said below
- w_zero: float32 [640, 640], replicated, may hold values from -0.25 to 0.25
- w_one_re: float32 [512, 512], replicated, may hold values from -0.1875 to 0.1875
- w_one_im: float32 [512, 512], replicated, may hold values from -0.1875 to 0.1875
- w_two_re: float32 [384, 384], replicated, may hold values from -0.21875 to 0.21875
- w_two_im: float32 [384, 384], replicated, may hold values from -0.21875 to 0.21875
Outputs:
- grad_feats: float32 [2, 2048, 3200], P('rep', ('src', 'tgt'))
- grad_w_zero: float32 [640, 640], P('src')
- grad_w_one_re: float32 [512, 512], P('src')
- grad_w_one_im: float32 [512, 512], P('src')
- grad_w_two_re: float32 [384, 384], P('src')
- grad_w_two_im: float32 [384, 384], P('src')
Inputs may be any that keep to these rules, and one draw needn't show every extreme that they name: `edge_count`: some tile of each structure is full.
All inputs are finite; a program needn't handle non-finite values.
Results may differ from a plain program's by a relative error of at most 0.0003.
Values sent between devices are 32-bit elements; how exact they have to be, the bound alone decides.
A program may use at most 128 MiB of HBM per device.

v0:
```python
import jax
import jax.numpy as jnp
from jax import lax
from jax.sharding import PartitionSpec as P

OFFSETS = (0, 1, 10, 35, 70)
HIGH = lax.Precision.HIGHEST


def rotations(wig):
    mats = []
    for level in range(5):
        order = min(level, 2)
        rows = 2 * order + 1
        cols = 2 * level + 1
        piece = wig[OFFSETS[level] : OFFSETS[level] + rows * cols]
        mats.append(piece.reshape(rows, cols, piece.shape[-1]))
    return mats


def group(rotated, count):
    zero = jnp.stack([rotated[v][:, min(v, 2)] for v in range(5)], 1)
    plus_one = jnp.stack([rotated[v][:, min(v, 2) + 1] for v in range(1, 5)], 1)
    minus_one = jnp.stack([rotated[v][:, min(v, 2) - 1] for v in range(1, 5)], 1)
    plus_two = jnp.stack([rotated[v][:, 4] for v in range(2, 5)], 1)
    minus_two = jnp.stack([rotated[v][:, 0] for v in range(2, 5)], 1)
    return tuple((a.reshape(count, -1) for a in (zero, plus_one, minus_one, plus_two, minus_two)))


def ungroup(groups, count, chans):
    zero, plus_one, minus_one, plus_two, minus_two = [a.reshape(count, -1, chans) for a in groups]
    result = []
    for level in range(5):
        rows = []
        if level >= 2:
            rows.append(minus_two[:, level - 2])
        if level >= 1:
            rows.append(minus_one[:, level - 1])
        rows.append(zero[:, level])
        if level >= 1:
            rows.append(plus_one[:, level - 1])
        if level >= 2:
            rows.append(plus_two[:, level - 2])
        result.append(jnp.stack(rows, 1))
    return result


def tdot(left, right):
    return lax.dot_general(
        left, right, (((0,), (0,)), ((), ())), precision=HIGH, preferred_element_type=jnp.float32
    )


def ntdot(left, right):
    return lax.dot_general(
        left, right, (((1,), (1,)), ((), ())), precision=HIGH, preferred_element_type=jnp.float32
    )


def block_grads(xrows, grows, wig, weights):
    w_zero, w_one_re, w_one_im, w_two_re, w_two_im = weights
    count, coefs, chans = xrows.shape
    mats = rotations(wig)
    xrot = [
        jnp.einsum("rcb,bcf->brf", mats[v], xrows[:, v * v : (v + 1) * (v + 1)], precision=HIGH)
        for v in range(5)
    ]
    grot = [
        jnp.einsum("rcb,bcf->brf", mats[v], grows[:, v * v : (v + 1) * (v + 1)], precision=HIGH)
        for v in range(5)
    ]
    z0, zp1, zm1, zp2, zm2 = group(xrot, count)
    u0, up1, um1, up2, um2 = group(grot, count)
    grads = (
        tdot(z0, u0),
        tdot(zp1, up1) + tdot(zm1, um1),
        tdot(zp1, um1) - tdot(zm1, up1),
        tdot(zp2, up2) + tdot(zm2, um2),
        tdot(zp2, um2) - tdot(zm2, up2),
    )
    d0 = ntdot(u0, w_zero)
    dp1 = ntdot(up1, w_one_re) + ntdot(um1, w_one_im)
    dm1 = ntdot(um1, w_one_re) - ntdot(up1, w_one_im)
    dp2 = ntdot(up2, w_two_re) + ntdot(um2, w_two_im)
    dm2 = ntdot(um2, w_two_re) - ntdot(up2, w_two_im)
    back = ungroup((d0, dp1, dm1, dp2, dm2), count, chans)
    pieces = [jnp.einsum("rcb,brf->bcf", mats[v], back[v], precision=HIGH) for v in range(5)]
    return (jnp.concatenate(pieces, 1), grads)


def local(
    src_feats,
    tgt_cotangent,
    rotation,
    edge_src,
    edge_tgt,
    edge_count,
    w_zero,
    w_one_re,
    w_one_im,
    w_two_re,
    w_two_im,
):
    weights = (w_zero, w_one_re, w_one_im, w_two_re, w_two_im)
    chans = w_zero.shape[0] // 5
    feat = src_feats.shape[2]
    source_block = lax.all_gather(src_feats, "tgt", axis=1, tiled=True)[0]
    target_block = lax.all_gather(tgt_cotangent, "src", axis=1, tiled=True)[0]
    src_blk = source_block.shape[0]
    source_block = source_block.reshape(src_blk, 25, chans)
    target_block = target_block.reshape(target_block.shape[0], 25, chans)
    sources = edge_src[0, 0, 0]
    targets = edge_tgt[0, 0, 0]
    wig = rotation[0, 0, 0]
    live_count = edge_count[0, 0, 0]
    cap = sources.shape[0]
    width = 128
    atom_ids = jnp.arange(src_blk, dtype=jnp.int32)

    def step(index, carry):
        total, sums = carry
        start = index * width
        src_ids = lax.dynamic_slice_in_dim(sources, start, width)
        tgt_ids = lax.dynamic_slice_in_dim(targets, start, width)
        wig_block = lax.dynamic_slice_in_dim(wig, start, width, 1)
        live = (start + jnp.arange(width, dtype=jnp.int32) < live_count).astype(jnp.float32)
        xrows = jnp.take(source_block, src_ids, axis=0) * live[:, None, None]
        grows = jnp.take(target_block, tgt_ids, axis=0) * live[:, None, None]
        term, parts = block_grads(xrows, grows, wig_block, weights)
        onehot = (src_ids[:, None] == atom_ids[None, :]).astype(jnp.float32)
        added = tdot(onehot, term.reshape(width, feat))
        return (total + added, tuple((a + b for a, b in zip(sums, parts))))

    stop = cap // width
    init = (
        jnp.zeros((src_blk, feat), jnp.float32),
        tuple((jnp.zeros(w.shape, jnp.float32) for w in weights)),
    )
    total, sums = lax.fori_loop(0, stop, step, init)
    grad_feats = lax.psum_scatter(total[None], "tgt", scatter_dimension=1, tiled=True)
    summed = lax.psum((sums[0], sums[1], sums[2], sums[3], sums[4]), ("rep", "src", "tgt"))
    owner = lax.axis_index("src")
    parts_count = lax.axis_size("src")
    final = tuple(
        (
            lax.dynamic_slice_in_dim(
                a, owner * (a.shape[0] // parts_count), a.shape[0] // parts_count, 0
            )
            for a in summed
        )
    )
    return (grad_feats, final[0], final[1], final[2], final[3], final[4])


def solution(mesh):
    placed = (
        P("rep", ("src", "tgt"), None),
        P("rep", ("tgt", "src"), None),
        P("rep", "src", "tgt", None, None),
        P("rep", "src", "tgt", None),
        P("rep", "src", "tgt", None),
        P("rep", "src", "tgt"),
        P(),
        P(),
        P(),
        P(),
        P(),
    )
    return jax.shard_map(
        local,
        mesh=mesh,
        in_specs=placed,
        out_specs=(
            P("rep", ("src", "tgt"), None),
            P("src", None),
            P("src", None),
            P("src", None),
            P("src", None),
            P("src", None),
        ),
        check_vma=False,
    )
```

profile of v0, /device:TPU:1, one launch (start us, length us, event | category | flops | bytes accessed | tf_op | source)
XLA Modules:
  0.0 846.4 jit_solution(5621229995447299344)
XLA Ops:
  7.2 1.8 copy.146
  9.1 1.8 copy.144
  13.4 68.2 %all-gather.5.cloned.1.call-done = f32[1,128,3200]{2,0,1:T(1,128)} async-done(((f32[1,16,3200]{2,0,1:T(1,128)}), f32[1,128,3200]{2,0,1:T(1,128)}) %all-gather.5.cloned.1.call-update) | async-done | bytes 1638416 | tf_op jit(solution)/shard_map/all_gather | solution.py:107
  81.6 3.4 copy.147
  85.0 2.2 copy.149
  87.2 72.5 %all-gather.3.cloned.1.call-done = f32[1,256,3200]{2,0,1:T(1,128)} async-done(((f32[1,16,3200]{2,0,1:T(1,128)}), f32[1,256,3200]{2,0,1:T(1,128)}) %all-gather.3.cloned.1.call-update) | async-done | bytes 3276816 | tf_op jit(solution)/shard_map/all_gather | solution.py:108
  159.7 6.0 copy.145
  165.7 3.7 copy.148
  169.4 296.7 %while.24 = (s32[]{:T(128)}, f32[128,3200]{1,0:T(8,128)}, f32[640,640]{1,0:T(8,128)}, f32[512,512]{1,0:T(8,128)}, f32[512,512]{1,0:T(8,128)}, /*index=5*/f32[384...) while((s32[]{:T(128)}, f32[128,3200]{1,0:T(8,128)}, ...), condition=%wide.region_1.0_spmd.clone, body=%wide.region_0.1_spmd.clone.sunk | while | flops 6995169280 | bytes 155906560 | solution.py:139
  170.2 2.3 gather_fusion.1
  185.4 2.9 gather_fusion
  194.2 1.6 fusion.278
  197.1 1.5 fusion.307
  200.5 1.7 pad_maximum_fusion.19
  203.3 2.6 fusion.308
  215.3 2.1 fusion.304
  223.1 2.6 select_add_fusion.2
  226.9 1.9 convolution_add_fusion.8
  228.8 1.8 copy.301
  230.6 3.7 fusion.286
  235.5 1.9 convolution_subtract_fusion.7
  246.0 2.1 fusion.292
  248.6 1.8 fusion.291
  250.9 1.8 fusion.290
  254.3 5.7 concatenate.9
  260.0 1.8 copy.309
  261.8 3.8 convolution_add_fusion.10
  266.8 2.3 gather_fusion.1
  282.0 2.9 gather_fusion
  296.7 1.7 pad_maximum_fusion.19
  299.5 2.8 fusion.308
  311.6 3.3 fusion.304
  320.6 4.1 select_add_fusion.2
  326.0 1.9 convolution_add_fusion.8
  327.9 1.8 copy.301
  329.7 3.7 fusion.286
  334.6 1.9 convolution_subtract_fusion.7
  345.1 2.2 fusion.292
  347.9 1.8 fusion.291
  350.2 1.8 fusion.290
  353.6 5.7 concatenate.9
  359.3 1.8 copy.309
  361.1 4.3 convolution_add_fusion.10
  366.4 2.3 gather_fusion.1
  381.6 2.9 gather_fusion
  392.9 1.5 fusion.307
  396.3 1.7 pad_maximum_fusion.19
  399.1 2.8 fusion.308
  411.2 3.3 fusion.304
  420.4 4.1 select_add_fusion.2
  425.7 1.9 convolution_add_fusion.8
  427.6 1.8 copy.301
  429.4 3.7 fusion.286
  434.4 1.9 convolution_subtract_fusion.7
  444.9 2.0 fusion.292
  447.4 1.8 fusion.291
  449.7 1.8 fusion.290
  453.1 5.7 concatenate.9
  458.8 1.8 copy.309
  460.6 4.3 convolution_add_fusion.10
  466.7 279.4 %all-reduce.3.cloned.1.call-done = (f32[640,640]{1,0:T(8,128)}, f32[512,512]{1,0:T(8,128)}, f32[512,512]{1,0:T(8,128)}, f32[384,384]{1,0:T(8,128)}, f32[384,384]{1,0:T(8,128)}) async-done(((f32[640,640]{1,0:T(8,128)}, f32[512,512]{1,0:T(8,128)}, f32[512,512]{1,0:T(8,128)}, f32[384,384]{1,0:T(8,128)}, f32[384,384]{1,0:T(8,128)}), (f32[640,640]{1,0:T(8,128)}, f32[512,512]{1,0:T(8,128)}, f32[512,512]{1,0:T(8,128)}, ...) | async-done | bytes 4915216 | tf_op jit(solution)/shard_map/psum | solution.py:141
  747.5 1.5 constant_dynamic-slice_fusion.4
  749.1 1.5 constant_dynamic-slice_fusion.2
  750.6 89.0 %reduce-scatter.2.cloned.1.call-done = f32[1,16,3200]{2,1,0:T(8,128)} async-done(((f32[1,128,3200]{2,1,0:T(8,128)}), f32[1,16,3200]{2,1,0:T(8,128)}) %reduce-scatter.2.cloned.1.call-update) | async-done | bytes 204816 | tf_op jit(solution)/shard_map/reduce_scatter | solution.py:140
  (633 shorter events, 163.5 us)
Async XLA Ops:
  7.2 74.4 %all-gather.5.cloned.1.call-start = ((), (), s32[]{:S(2)}) async-start(), calls=%async_computation.2 | async-start | bytes 1843200 | tf_op jit(solution)/shard_map/all_gather | solution.py:107
  9.1 150.6 %all-gather.3.cloned.1.call-start = ((), (), s32[]{:S(2)}) async-start(), calls=%async_computation.1 | async-start | bytes 3481600 | tf_op jit(solution)/shard_map/all_gather | solution.py:108
  11.0 735.2 %all-reduce.3.cloned.1.call-start = ((), (), s32[]{:S(2)}) async-start(), calls=%async_computation.4 | async-start | bytes 9830400 | tf_op jit(solution)/shard_map/psum | solution.py:141
  169.4 5.5 copy-start.48
  169.4 15.9 %copy-start.52 = (s32[384]{0:T(512)}, s32[384]{0:T(512)S(1)}, u32[]{:S(2)}) copy-start(s32[384]{0:T(512)S(1)} %get-tuple-element.817) | copy-start | bytes 4612 | tf_op jit(solution)/shard_map/while
  175.2 3.9 slice-start
  179.1 3.8 copy-start.2
  179.2 3.8 slice-start.1
  197.1 3.4 copy-start.23
  203.3 3.3 copy-start.15
  206.6 3.8 copy-start.34
  209.2 4.2 copy-start.38
  209.2 4.2 copy-start.40
  209.2 4.2 copy-start.41
  211.6 3.1 copy-start.32
  211.6 3.1 copy-start.33
  211.6 3.1 copy-start.35
  235.5 3.0 copy-start.10
  235.5 3.8 copy-start.9
  250.9 3.2 copy-start.30
  261.8 3.8 copy-start.49
  261.8 3.8 copy-start.51
  261.8 3.8 copy-start.53
  266.0 5.5 copy-start.48
  266.0 15.9 %copy-start.52 = (s32[384]{0:T(512)}, s32[384]{0:T(512)S(1)}, u32[]{:S(2)}) copy-start(s32[384]{0:T(512)S(1)} %get-tuple-element.817) | copy-start | bytes 4612 | tf_op jit(solution)/shard_map/while
  271.8 3.9 slice-start
  275.7 3.8 copy-start.2
  275.8 3.8 slice-start.1
  293.3 3.4 copy-start.23
  299.5 3.5 copy-start.15
  303.0 3.8 copy-start.34
  305.6 4.2 copy-start.38
  305.6 4.2 copy-start.40
  305.6 4.2 copy-start.41
  307.9 3.1 copy-start.32
  307.9 3.1 copy-start.33
  308.0 3.1 copy-start.35
  320.6 4.1 copy-start.7
  334.6 3.8 copy-start.9
  350.2 3.2 copy-start.30
  361.1 4.3 copy-start.49
  361.1 4.3 copy-start.51
  361.1 4.3 copy-start.53
  365.6 5.5 copy-start.48
  365.6 15.9 %copy-start.52 = (s32[384]{0:T(512)}, s32[384]{0:T(512)S(1)}, u32[]{:S(2)}) copy-start(s32[384]{0:T(512)S(1)} %get-tuple-element.817) | copy-start | bytes 4612 | tf_op jit(solution)/shard_map/while
  371.4 3.9 slice-start
  375.3 3.8 copy-start.2
  375.3 3.8 slice-start.1
  392.9 3.4 copy-start.23
  399.1 3.5 copy-start.15
  402.6 3.8 copy-start.34
  405.2 4.2 copy-start.38
  405.2 4.2 copy-start.40
  405.2 4.2 copy-start.41
  407.5 3.1 copy-start.32
  407.6 3.1 copy-start.33
  407.6 3.1 copy-start.35
  420.4 4.1 copy-start.7
  434.4 3.8 copy-start.9
  449.7 3.2 copy-start.30
  460.6 4.3 copy-start.49
  460.6 4.3 copy-start.51
  460.6 4.3 copy-start.53
  466.1 373.5 %reduce-scatter.2.cloned.1.call-start = ((), (), s32[]{:S(2)}) async-start(), calls=%async_computation.3 | async-start | bytes 1843200 | tf_op jit(solution)/shard_map/reduce_scatter | solution.py:140
  (111 other events, 210.4 us)
Sparse Core Ops, SparseCore 0:
  10.6 70.9 all-gather.4
  83.9 75.7 all-gather.2
  466.2 279.8 all-reduce.2
  750.6 88.9 reduce-scatter.1
where the time goes:
time: 852 us; the launch traced here: 846 us
  waiting for transfers between devices  510 us (60%)
  local copies, waits for them, and re-layouts  145 us (17%)
  matrix products  144 us (17%)
  other arithmetic  28.3 us (3%)
  between operations  14.1 us (2%)
    psum x1, waiting for transfers between devices, local(): lax.psum((sums[0], sums[1], sums[2], sums[3], sums[4]), ('rep', 'src', 't...  279 us
    reduce_scatter x1, waiting for transfers between devices, local(): lax.psum_scatter(total[None], 'tgt', scatter_dimension=1, tiled=True)  89 us
    all_gather x1, waiting for transfers between devices, local(): target_block = lax.all_gather(tgt_cotangent, 'src', axis=1, tiled=True)[0]  72.5 us
    all_gather x1, waiting for transfers between devices, local(): source_block = lax.all_gather(src_feats, 'tgt', axis=1, tiled=True)[0]  68.2 us
    dot_general x30, matrix products, tdot(): lax.dot_general(left, right, (((0,), (0,)), ((), ())), precision=HIGH, pr...  58.3 us
    dot_general x27, matrix products, ntdot(): lax.dot_general(left, right, (((1,), (1,)), ((), ())), precision=HIGH, pr...  39.2 us
    while x357, local copies, waits for them, and re-layouts  25.1 us
    concatenate x6, local copies, waits for them, and re-layouts, block_grads(): return (jnp.concatenate(pieces, 1), grads)  22.6 us
  transfers between devices with their start and end apart: 4, of which 4 were waited for; matrix products, arithmetic and copies ran while one was open for 2% of the time, Pallas kernels for 0%

commit v1 on v0

v1 whole, which is shorter than its diff:
```python
import jax
import jax.numpy as jnp
from jax import lax
from jax.experimental import pallas as pl
from jax.experimental.pallas import tpu as pltpu
from jax.sharding import PartitionSpec as P

OFFSETS = (0, 1, 10, 35, 70)
F32, BF16 = jnp.float32, jnp.bfloat16
NT = (((1,), (1,)), ((), ()))
NN = (((1,), (0,)), ((), ()))


def mm(a, b, dims):
    return lax.dot_general(a, b, dims, preferred_element_type=F32)


def split(a):
    hi = a.astype(BF16)
    return hi, (a - hi.astype(F32)).astype(BF16)


def onehot(ids, live, atoms):
    rows = lax.broadcasted_iota(jnp.int32, (atoms, ids.shape[1]), 0)
    return jnp.where((rows == ids) & live, 1.0, 0.0).astype(BF16)


def pick(block_ref, hot_ref, out_ref, chans):
    def one(c, carry):
        at = pl.multiple_of(c * chans, chans)
        hi, lo = split(block_ref[:, pl.ds(at, chans)].T)
        out_ref[pl.ds(at, chans), :] = mm(jnp.concatenate([hi, lo], 1), hot_ref[...], NN)
        return carry

    lax.fori_loop(0, out_ref.shape[0] // chans, one, 0)


def rotate(rows_ref, rot_ref, put, chans, cap):
    steps, lanes = 16, 128
    tiles = cap // lanes

    def one(i, carry):
        ch = pl.multiple_of((i // tiles) * steps, steps)
        ln = pl.multiple_of((i % tiles) * lanes, lanes)
        for level in range(5):
            q, cols = min(level, 2), 2 * level + 1
            xs = [
                rows_ref[pl.ds((level * level + c) * chans + ch, steps), pl.ds(ln, lanes)]
                for c in range(cols)
            ]
            for r in range(2 * q + 1):
                acc = None
                for c in range(cols):
                    o = OFFSETS[level] + r * cols + c
                    term = rot_ref[o : o + 1, pl.ds(ln, lanes)] * xs[c]
                    acc = term if acc is None else acc + term
                m = r - q
                put(abs(m), m < 0, level - abs(m), ch, ln, acc)
        return carry

    lax.fori_loop(0, (chans // steps) * tiles, one, 0)


def compute_kernel(
    cnt_ref, x_ref, g_ref, rot_ref, es_ref, et_ref,
    w0_ref, w1r_ref, w1i_ref, w2r_ref, w2i_ref,
    total_ref, wg_ref,
    hs_ref, ht_ref, hs2_ref, rows_ref,
    z0_ref, z1_ref, z2_ref, u0_ref, u1_ref, u2_ref, v1_ref, v2_ref,
    wh0, wh1r, wh1i, wh2r, wh2i, d0_ref, d1_ref, d2_ref, term_ref,
):
    cap = es_ref.shape[1]
    chans = w0_ref.shape[0] // 5
    src_blk, tgt_blk = x_ref.shape[0], g_ref.shape[0]
    live = lax.broadcasted_iota(jnp.int32, (1, cap), 1) < cnt_ref[0]
    hot = onehot(es_ref[...], live, src_blk)
    hs_ref[:src_blk, :] = hot
    hs_ref[src_blk:, :] = hot
    hs2_ref[:, :cap] = hot
    hs2_ref[:, cap:] = hot
    hot = onehot(et_ref[...], live, tgt_blk)
    ht_ref[:tgt_blk, :] = hot
    ht_ref[tgt_blk:, :] = hot

    zrefs = (z0_ref, z1_ref, z2_ref)

    def put_z(order, neg, k, ch, ln, val):
        hi, lo = split(val)
        rows = pl.ds(k * chans + ch, 16)
        at = pl.ds(ln + (cap if neg else 0), 128)
        zrefs[order][0, rows, at] = hi
        zrefs[order][1, rows, at] = lo

    pick(x_ref, hs_ref, rows_ref, chans)
    rotate(rows_ref, rot_ref, put_z, chans, cap)

    urefs = (u0_ref, u1_ref, u2_ref)
    vrefs = (None, v1_ref, v2_ref)

    def put_u(order, neg, k, ch, ln, val):
        hi, lo = split(val)
        rows = pl.ds(k * chans + ch, 16)
        at = pl.ds(ln + (cap if neg else 0), 128)
        urefs[order][0, rows, at] = hi
        urefs[order][1, rows, at] = lo
        if order:
            at = pl.ds(ln + (0 if neg else cap), 128)
            vrefs[order][0, rows, at] = hi if neg else -hi
            vrefs[order][1, rows, at] = lo if neg else -lo

    pick(g_ref, ht_ref, rows_ref, chans)
    rotate(rows_ref, rot_ref, put_u, chans, cap)

    def grad(z, u, at, count):
        zh, zl = z[0, pl.ds(at, count), :], z[1, pl.ds(at, count), :]
        return mm(zh, u[0], NT) + mm(zh, u[1], NT) + mm(zl, u[0], NT)

    owners = wg_ref.shape[0]
    half = owners // 2

    def grads(h, carry):
        base = 0
        for z, u, cols in (
            (z0_ref, u0_ref, 5), (z1_ref, u1_ref, 4), (z1_ref, v1_ref, 4), (z2_ref, u2_ref, 3), (z2_ref, v2_ref, 3),
        ):
            per = cols * chans // owners
            res = grad(z, u, pl.multiple_of(h * half * per, 16), half * per)
            for s in range(half):
                for j in range(cols):
                    wg_ref[h * half + s, base + j * per : base + (j + 1) * per, :] = res[
                        s * per : (s + 1) * per, j * chans : (j + 1) * chans
                    ]
            base += cols * per
        return carry

    lax.fori_loop(0, 2, grads, 0)

    for src, dst in ((w0_ref, wh0), (w1r_ref, wh1r), (w1i_ref, wh1i), (w2r_ref, wh2r), (w2i_ref, wh2i)):
        def cut(i, carry, src=src, dst=dst):
            at = pl.ds(pl.multiple_of(i * 128, 128), 128)
            dst[0, at, :], dst[1, at, :] = split(src[at, :])
            return carry

        lax.fori_loop(0, src.shape[0] // 128, cut, 0)

    def three(w, u, at):
        wh, wl = w[0, at, :], w[1, at, :]
        return mm(wh, u[0], NN) + mm(wh, u[1], NN) + mm(wl, u[0], NN)

    for at in (pl.ds(0, 320), pl.ds(320, 320)):
        d0_ref[at, :] = three(wh0, u0_ref, at)
    for at in (pl.ds(0, 256), pl.ds(256, 256)):
        d1_ref[at, :] = three(wh1r, u1_ref, at) + three(wh1i, v1_ref, at)
    for at in (pl.ds(0, 192), pl.ds(192, 192)):
        d2_ref[at, :] = three(wh2r, u2_ref, at) + three(wh2i, v2_ref, at)

    drefs = (d0_ref, d1_ref, d2_ref)
    tiles = cap // 128

    def back(i, carry):
        ch = pl.multiple_of((i // tiles) * 16, 16)
        ln = pl.multiple_of((i % tiles) * 128, 128)
        for level in range(5):
            q, cols = min(level, 2), 2 * level + 1
            ds = []
            for r in range(2 * q + 1):
                m = r - q
                k = level - abs(m)
                ds.append(drefs[abs(m)][pl.ds(k * chans + ch, 16), pl.ds(ln + (cap if m < 0 else 0), 128)])
            for c in range(cols):
                acc = None
                for r in range(2 * q + 1):
                    o = OFFSETS[level] + r * cols + c
                    term = rot_ref[o : o + 1, pl.ds(ln, 128)] * ds[r]
                    acc = term if acc is None else acc + term
                hi, lo = split(acc)
                rows = pl.ds((level * level + c) * chans + ch, 16)
                term_ref[rows, pl.ds(ln, 128)] = hi
                term_ref[rows, pl.ds(ln + cap, 128)] = lo
        return carry

    lax.fori_loop(0, (chans // 16) * tiles, back, 0)

    def scatter(c, carry):
        at = pl.multiple_of(c * 5 * chans, chans)
        total_ref[:, pl.ds(at, 5 * chans)] = mm(hs2_ref[...], term_ref[pl.ds(at, 5 * chans), :], NT)
        return carry

    lax.fori_loop(0, 5, scatter, 0)


def compute(xb, gb, wig, es, et, cnt, weights, owners):
    cap = es.shape[1]
    chans = weights[0].shape[0] // 5
    src_blk, feat = xb.shape
    tgt_blk = gb.shape[0]
    per = 600
    vm = pl.BlockSpec(memory_space=pltpu.VMEM)
    dims = [w.shape[0] for w in weights]
    scratch = [
        pltpu.VMEM((2 * src_blk, cap), BF16),
        pltpu.VMEM((2 * tgt_blk, cap), BF16),
        pltpu.VMEM((src_blk, 2 * cap), BF16),
        pltpu.VMEM((feat, cap), F32),
        pltpu.VMEM((2, dims[0], cap), BF16),
        pltpu.VMEM((2, dims[1], 2 * cap), BF16),
        pltpu.VMEM((2, dims[3], 2 * cap), BF16),
        pltpu.VMEM((2, dims[0], cap), BF16),
        pltpu.VMEM((2, dims[1], 2 * cap), BF16),
        pltpu.VMEM((2, dims[3], 2 * cap), BF16),
        pltpu.VMEM((2, dims[1], 2 * cap), BF16),
        pltpu.VMEM((2, dims[3], 2 * cap), BF16),
        *[pltpu.VMEM((2, d, d), BF16) for d in dims],
        pltpu.VMEM((dims[0], cap), F32),
        pltpu.VMEM((dims[1], 2 * cap), F32),
        pltpu.VMEM((dims[3], 2 * cap), F32),
        pltpu.VMEM((feat, 2 * cap), BF16),
    ]
    return pl.pallas_call(
        compute_kernel,
        out_shape=(
            jax.ShapeDtypeStruct((src_blk, feat), F32),
            jax.ShapeDtypeStruct((owners, per, chans), F32),
        ),
        in_specs=[pl.BlockSpec(memory_space=pltpu.SMEM)] + [vm] * 10,
        out_specs=(vm, vm),
        scratch_shapes=scratch,
        compiler_params=pltpu.CompilerParams(vmem_limit_bytes=60 * 2**20),
        name="tile",
    )(cnt, xb, gb, wig, es, et, *weights)


def unpack(packed, weights, owners, chans):
    outs, base = [], 0
    for w in weights:
        cols = w.shape[0] // chans
        per = w.shape[0] // owners
        piece = packed[base : base + cols * per].reshape(cols, per, chans)
        outs.append(piece.transpose(1, 0, 2).reshape(per, cols * chans))
        base += cols * per
    return outs


def local(src_feats, tgt_cotangent, rotation, edge_src, edge_tgt, edge_count, *weights):
    chans = weights[0].shape[0] // 5
    owners = lax.axis_size("src")
    xb = lax.all_gather(src_feats[0], "tgt", axis=0, tiled=True)
    gb = lax.all_gather(tgt_cotangent[0], "src", axis=0, tiled=True)
    total, wg = compute(
        xb, gb, rotation[0, 0, 0], edge_src[0, 0], edge_tgt[0, 0], edge_count[0, 0], weights, owners
    )
    part = lax.psum_scatter(wg, "src", scatter_dimension=0, tiled=True)[0]
    grad_feats = lax.psum_scatter(total[None], "tgt", scatter_dimension=1, tiled=True)
    packed = lax.psum(part, ("rep", "tgt"))
    return (grad_feats, *unpack(packed, weights, owners, chans))


def solution(mesh):
    placed = (
        P("rep", ("src", "tgt"), None),
        P("rep", ("tgt", "src"), None),
        P("rep", "src", "tgt", None, None),
        P("rep", "src", "tgt", None),
        P("rep", "src", "tgt", None),
        P("rep", "src", "tgt"),
        P(), P(), P(), P(), P(),
    )
    return jax.shard_map(
        local,
        mesh=mesh,
        in_specs=placed,
        out_specs=(P("rep", ("src", "tgt"), None), *[P("src", None)] * 5),
        check_vma=False,
    )
```

time: 852 us -> 591 us (0.69)
  matrix products: 144 us -> 0 us
  local copies, waits for them, and re-layouts: 145 us -> 6.2 us
  Pallas kernels: 0 us -> 42.7 us
  other arithmetic: 28.3 us -> 0 us
  waiting for transfers between devices: 510 us -> 527 us
    dot_general x93 -> x0, matrix products: 144 us -> none  [the longest x30 58.3 us: tdot(): lax.dot_general(left, right, (((0,), (0,)), ((), ())), precision=HIGH, pr...]
    unnamed x4 -> x6, waiting for transfers between devices: 0.57 us -> 96.6 us
    psum x1, waiting for transfers between devices: 279 us -> 190 us  [local(): packed = lax.psum(part, ('rep', 'tgt'))]
    pallas_call x0 -> x1, Pallas kernels: none -> 42.7 us  [compute(): pl.pallas_call(compute_kernel, out_shape=(jax.ShapeDtypeStruct((src_blk,...]
    while x357 -> x0, local copies, waits for them, and re-layouts: 25.1 us -> none
    slice x60 -> x3, local copies, waits for them, and re-layouts: 27.7 us -> 2.57 us  [unpack(): piece = packed[base:base + cols * per].reshape(cols, per, chans)]
    concatenate x6 -> x0, local copies, waits for them, and re-layouts: 22.6 us -> none  [block_grads(): return (jnp.concatenate(pieces, 1), grads)]
    gather x6 -> x0, local copies, waits for them, and re-layouts: 15.4 us -> none  [the longest x3 8.61 us: step(): grows = jnp.take(target_block, tgt_ids, axis=0) * live[:, None, None]]
  transfers between devices with their start and end apart: 4 -> 5, of which waited for: 4 -> 5; matrix products, arithmetic and copies ran while one was open for 2% -> 1% of each run, Pallas kernels for 0% -> 0%
where the time goes in v1:
time: 591 us
  waiting for transfers between devices  527 us (89%)
  Pallas kernels  42.7 us (7%)
  between operations  14.4 us (2%)
  local copies, waits for them, and re-layouts  6.2 us (1%)
    psum x1, waiting for transfers between devices, local(): packed = lax.psum(part, ('rep', 'tgt'))  190 us
    unnamed x6, waiting for transfers between devices  96.6 us
    reduce_scatter x1, waiting for transfers between devices, local(): lax.psum_scatter(total[None], 'tgt', scatter_dimension=1, tiled=True)  92.5 us
    all_gather x1, waiting for transfers between devices, local(): gb = lax.all_gather(tgt_cotangent[0], 'src', axis=0, tiled=True)  77.5 us
    all_gather x1, waiting for transfers between devices, local(): xb = lax.all_gather(src_feats[0], 'tgt', axis=0, tiled=True)  70.6 us
    pallas_call x1, Pallas kernels, compute(): pl.pallas_call(compute_kernel, out_shape=(jax.ShapeDtypeStruct((src_blk,...  42.7 us
  transfers between devices with their start and end apart: 5, of which 5 were waited for; matrix products, arithmetic and copies ran while one was open for 1% of the time, Pallas kernels for 0%

profile of v1, /device:TPU:1, one launch (start us, length us, event | category | flops | bytes accessed | tf_op | source)
XLA Modules:
  0.0 590.6 jit_solution(4000106594876701747)
XLA Ops:
  7.2 0.0 all-gather.5.cloned.1.call-start
  7.2 0.7 all-gather.5.cloned.1.call-update
  7.9 0.0 all-gather.7.cloned.1.call-start
  7.9 0.7 all-gather.7.cloned.1.call-update
  8.7 0.0 reduce-scatter.8.cloned.1.call-start
  9.3 1.6 copy.44
  10.9 70.6 %all-gather.5.cloned.1.call-done = f32[1,128,3200]{2,1,0:T(8,128)} async-done(((f32[1,16,3200]{2,1,0:T(8,128)}), f32[1,128,3200]{2,1,0:T(8,128)}) %all-gather.5.cloned.1.call-update) | async-done | bytes 1638416 | tf_op jit(solution)/shard_map/all_gather | solution.py:247
  81.6 77.5 %all-gather.7.cloned.1.call-done = f32[1,256,3200]{2,1,0:T(8,128)} async-done(((f32[1,16,3200]{2,1,0:T(8,128)}), f32[1,256,3200]{2,1,0:T(8,128)}) %all-gather.7.cloned.1.call-update) | async-done | bytes 3276816 | tf_op jit(solution)/shard_map/all_gather | solution.py:248
  159.1 42.7 %tile.1 = (f32[128,3200]{1,0:T(8,128)}, f32[16,600,128]{2,1,0:T(8,128)}) custom-call(s32[1]{0:T(128)} %bitcast.39.cnt_ref, f32[128,3200]{1,0:T(8,128)} %bitcast.42, f32[256,3200]{1,0:T(8,128)} %bitcast.40, f32[115,384]{1,0:T(8,128)} %bitcast.43, s32[1,384]{1,0:T(1,128)} %bitcast.54, s32[1,384]{1,0:T(1,128)} %bitcast.55, f32[640,640]{1,0:T(8,128)} %w0_ref.1, ...), custom_call_target="tpu_custom_call" | custom-call | tf_op jit(solution)/shard_map/tile/pallas_call | solution.py:219
  201.8 0.0 reduce-scatter.8.cloned.1.call-update
  201.9 0.0 all-reduce.3.cloned.1.call-start
  201.9 94.7 %reduce-scatter.8.cloned.1.call-done = f32[1,600,128]{2,1,0:T(8,128)} async-done(((f32[16,600,128]{2,1,0:T(8,128)}), f32[1,600,128]{2,1,0:T(8,128)}) %reduce-scatter.8.cloned.1.call-update) | async-done | bytes 307216
  296.6 0.0 all-reduce.3.cloned.1.call-update
  296.6 0.0 reduce-scatter.6.cloned.1.call-start
  296.7 0.5 reduce-scatter.6.cloned.1.call-update
  297.2 189.7 %all-reduce.3.cloned.1.call-done = f32[600,128]{1,0:T(8,128)} async-done(((f32[600,128]{1,0:T(8,128)}), f32[600,128]{1,0:T(8,128)}) %all-reduce.3.cloned.1.call-update) | async-done | bytes 307216 | tf_op jit(solution)/shard_map/psum | solution.py:254
  486.9 0.8 fusion
  487.8 0.9 slice.20
  488.7 0.7 copy.45
  489.4 0.6 copy_bitcast_fusion.4
  490.0 0.9 fusion.1
  490.9 0.7 copy_bitcast_fusion.2
  491.5 92.5 %reduce-scatter.6.cloned.1.call-done = f32[1,16,3200]{2,1,0:T(8,128)} async-done(((f32[1,128,3200]{2,1,0:T(8,128)}), f32[1,16,3200]{2,1,0:T(8,128)}) %reduce-scatter.6.cloned.1.call-update) | async-done | bytes 204816 | tf_op jit(solution)/shard_map/reduce_scatter | solution.py:253
  (3 shorter events, 0.1 us)
Async XLA Ops:
  7.2 74.4 %all-gather.5.cloned.1.call-start = ((), (), s32[]{:S(2)}) async-start(), calls=%async_computation.4 | async-start | bytes 1843200 | tf_op jit(solution)/shard_map/all_gather | solution.py:247
  7.9 151.2 %all-gather.7.cloned.1.call-start = ((), (), s32[]{:S(2)}) async-start(), calls=%async_computation.5 | async-start | bytes 3481600 | tf_op jit(solution)/shard_map/all_gather | solution.py:248
  8.7 287.9 %reduce-scatter.8.cloned.1.call-start = ((), (), s32[]{:S(2)}) async-start(), calls=%async_computation.6 | async-start | bytes 5222400
  201.9 285.1 %all-reduce.3.cloned.1.call-start = ((), (), s32[]{:S(2)}) async-start(), calls=%async_computation.3 | async-start | bytes 614400 | tf_op jit(solution)/shard_map/psum | solution.py:254
  296.6 287.4 %reduce-scatter.6.cloned.1.call-start = ((), (), s32[]{:S(2)}) async-start(), calls=%async_computation.2 | async-start | bytes 1843200 | tf_op jit(solution)/shard_map/reduce_scatter | solution.py:253
Sparse Core Ops, SparseCore 0:
  10.6 70.9 all-gather.4
  83.4 75.7 all-gather.6
  202.0 94.5 reduce-scatter.7
  299.3 187.6 all-reduce.2
  491.4 92.5 reduce-scatter.5

commit v2 on v1

--- a/solution.py
+++ b/solution.py
@@ -7,6 +7,8 @@
 
 OFFSETS = (0, 1, 10, 35, 70)
 F32, BF16 = jnp.float32, jnp.bfloat16
+MESH = pl.DeviceIdType.MESH
+PACK = 640
 NT = (((1,), (1,)), ((), ()))
 NN = (((1,), (0,)), ((), ()))
 
@@ -131,6 +133,7 @@
                         s * per : (s + 1) * per, j * chans : (j + 1) * chans
                     ]
             base += cols * per
+        wg_ref[pl.ds(h * half, half), base:, :] = jnp.zeros((half, wg_ref.shape[1] - base, chans), F32)
         return carry
 
     lax.fori_loop(0, 2, grads, 0)
@@ -194,7 +197,7 @@
     chans = weights[0].shape[0] // 5
     src_blk, feat = xb.shape
     tgt_blk = gb.shape[0]
-    per = 600
+    per = PACK
     vm = pl.BlockSpec(memory_space=pltpu.VMEM)
     dims = [w.shape[0] for w in weights]
     scratch = [
@@ -230,29 +233,317 @@
     )(cnt, xb, gb, wig, es, et, *weights)
 
 
-def unpack(packed, weights, owners, chans):
-    outs, base = [], 0
-    for w in weights:
-        cols = w.shape[0] // chans
-        per = w.shape[0] // owners
-        piece = packed[base : base + cols * per].reshape(cols, per, chans)
-        outs.append(piece.transpose(1, 0, 2).reshape(per, cols * chans))
-        base += cols * per
+def place():
+    rep, src, tgt = lax.axis_index("rep"), lax.axis_index("src"), lax.axis_index("tgt")
+    return rep, src // 4, src % 4, tgt // 4, tgt % 4
+
+
+def device(rep, zl, x, zh, y):
+    return (rep, zl * 4 + x, zh * 4 + y)
+
+
+def pair(i, d):
+    return (i + 1 - 2 * (i % 2), (i + 2) % 4, 3 - i)[d - 1]
+
+
+class Copies:
+    def __init__(self, send, recv):
+        self.send, self.recv, self.made = send, recv, []
+
+    def start(self, src, dst, to):
+        n = len(self.made)
+        copy = pltpu.make_async_remote_copy(
+            src_ref=src, dst_ref=dst, send_sem=self.send.at[n], recv_sem=self.recv.at[n],
+            device_id=to, device_id_type=MESH,
+        )
+        copy.start()
+        self.made.append(copy)
+        return copy
+
+    def drain(self):
+        for copy in self.made:
+            copy.wait_send()
+
+
+def greet(peers):
+    barrier = pltpu.get_barrier_semaphore()
+    for peer in peers:
+        pl.semaphore_signal(barrier, inc=1, device_id=peer, device_id_type=MESH)
+    pl.semaphore_wait(barrier, len(peers))
+
+
+def gather_kernel(x_in, g_in, x_out, g_out, send, recv, own):
+    rep, zl, x, zh, y = place()
+    right, left = (x + 1) % 4, (x + 3) % 4
+    up, down = (y + 1) % 4, (y + 3) % 4
+    lines = [pair(zl, d) for d in (1, 2, 3)]
+
+    def on_x(nx):
+        return device(rep, zl, nx, zh, y)
+
+    def on_y(ny):
+        return device(rep, zl, x, zh, ny)
+
+    def on_z(nz):
+        return device(rep, nz, x, zh, y)
+
+    across = device(rep, zl, x, 1 - zh, y)
+    greet([*[on_z(p) for p in lines], on_x(left), on_x(right), on_y(down), on_y(up), across])
+    far = Copies(send, recv)
+    mine_g, mine_x = zl * 4 + x, zh * 4 + y
+    zs = [far.start(g_in, g_out.at[mine_g], on_z(p)) for p in lines]
+    hop = far.start(x_in, x_out.at[mine_x], across)
+
+    def both(ref, slot, out, to, one, other):
+        return (
+            far.start(ref, out.at[slot], to(one)),
+            far.start(ref, out.at[slot], to(other)),
+        )
+
+    def relay(copies, out, slots, to, one, other):
+        copies[0].wait_recv()
+        a = far.start(out.at[slots[0], :8], out.at[slots[0], :8], to(one))
+        copies[1].wait_recv()
+        b = far.start(out.at[slots[1], 8:], out.at[slots[1], 8:], to(other))
+        return a, b
+
+    xs = [both(g_in, mine_g, g_out, on_x, right, left)]
+    ys = [both(x_in, mine_x, x_out, on_y, up, down)]
+    keep = [
+        pltpu.make_async_copy(g_in, g_out.at[mine_g], own.at[0]),
+        pltpu.make_async_copy(x_in, x_out.at[mine_x], own.at[1]),
+    ]
+    for copy in keep:
+        copy.start()
+    ends = []
+    order = [zl, *lines]
+
+    def x_step(j):
+        zs[j - 1].wait_recv()
+        slot = order[j] * 4 + x
+        xs.append(both(g_out.at[slot], slot, g_out, on_x, right, left))
+
+    def x_relay(j):
+        ends.extend(relay(xs[j], g_out, (order[j] * 4 + left, order[j] * 4 + right), on_x, right, left))
+
+    def y_relay(j):
+        at = (zh, 1 - zh)[j] * 4
+        ends.extend(relay(ys[j], x_out, (at + down, at + up), on_y, up, down))
+
+    x_step(1)
+    x_relay(0)
+    y_relay(0)
+    x_step(2)
+    x_relay(1)
+    hop.wait_recv()
+    slot = (1 - zh) * 4 + y
+    ys.append(both(x_out.at[slot], slot, x_out, on_y, up, down))
+    x_step(3)
+    x_relay(2)
+    y_relay(1)
+    x_relay(3)
+    for copy in ends:
+        copy.wait_recv()
+    for copy in keep:
+        copy.wait()
+    far.drain()
+
+
+def gather(src_feats, tgt_cotangent, n_src, n_tgt):
+    rows, feat = src_feats.shape
+    vm = pl.BlockSpec(memory_space=pltpu.VMEM)
+    count = 28
+    return pl.pallas_call(
+        gather_kernel,
+        out_shape=(
+            jax.ShapeDtypeStruct((n_tgt, rows, feat), F32),
+            jax.ShapeDtypeStruct((n_src, rows, feat), F32),
+        ),
+        in_specs=[vm, vm],
+        out_specs=(vm, vm),
+        scratch_shapes=[
+            pltpu.SemaphoreType.DMA((count,)),
+            pltpu.SemaphoreType.DMA((count,)),
+            pltpu.SemaphoreType.DMA((2,)),
+        ],
+        compiler_params=pltpu.CompilerParams(
+            collective_id=0, has_side_effects=True, vmem_limit_bytes=40 * 2**20
+        ),
+        name="spread",
+    )(src_feats, tgt_cotangent)
+
+
+def ring_first(far, me, part, hops, to):
+    right, left, opp = (me + 1) % 4, (me + 3) % 4, (me + 2) % 4
+    return (
+        far.start(part(opp, 0), hops.at[0], to(right)),
+        far.start(part(opp, 1), hops.at[1], to(left)),
+    )
+
+
+def ring_rest(far, me, part, firsts, hops, ins, to):
+    right, left = (me + 1) % 4, (me + 3) % 4
+    made = [
+        far.start(part(right, 1), ins.at[0, 1], to(right)),
+        far.start(part(left, 0), ins.at[1, 0], to(left)),
+    ]
+    firsts[0].wait_recv()
+    hops[0] = hops[0] + part(right, 0)[...]
+    made.append(far.start(hops.at[0], ins.at[0, 0], to(right)))
+    firsts[1].wait_recv()
+    hops[1] = hops[1] + part(left, 1)[...]
+    made.append(far.start(hops.at[1], ins.at[1, 1], to(left)))
+    return made
+
+
+def reduce_kernel(
+    total, wg, out, o0, o1, o2, o3, o4,
+    f_hops, f_ins, f_mine, f_got, halves, acc, x_hops, x_ins, w1, y_hops, y_ins, w2, z_got, packed, send, recv,
+):
+    rep, zl, x, zh, y = place()
+    other = device(1 - rep, zl, x, zh, y)
+
+    def on_x(nx):
+        return device(rep, zl, nx, zh, y)
+
+    def on_y(ny):
+        return device(rep, zl, x, zh, ny)
+
+    zs = [(pair(zl, d) if d else zl, (1 - zh) if far_z else zh) for far_z in (0, 1) for d in range(4)][1:]
+    ags = [((rep + dr) % 2, (y + dy) % 4) for dr in (0, 1) for dy in range(4)][1:]
+    greet(
+        [on_x((x + 1) % 4), on_x((x + 3) % 4)]
+        + [device(rep, a, x, b, y) for a, b in zs]
+        + [device(a, zl, x, zh, b) for a, b in ags]
+    )
+    far = Copies(send, recv)
+    swaps = []
+    xorder = [(x + 2) % 4, (x + 1) % 4, (x + 3) % 4, x]
+    for nx in xorder:
+        swaps.append(far.start(wg.at[:, nx, pl.ds(4 * (1 - rep), 4)], halves.at[:, nx], other))
+
+    def f_part(ny, h):
+        return total.at[:, ny, pl.ds(8 * h, 8)]
+
+    f_first = ring_first(far, y, f_part, f_hops, on_y)
+
+    def fold(i):
+        swaps[i].wait_recv()
+        nx = xorder[i]
+        acc[:, nx] = wg[:, nx, pl.ds(4 * rep, 4)] + halves[:, nx]
+
+    def x_part(nx, h):
+        return acc.at[:, nx, pl.ds(2 * h, 2)]
+
+    fold(0)
+    x_first = ring_first(far, x, x_part, x_hops, on_x)
+    fold(1)
+    fold(2)
+    f_rest = ring_rest(far, y, f_part, f_first, f_hops, f_ins, on_y)
+    x_rest = ring_rest(far, x, x_part, x_first, x_hops, x_ins, on_x)
+    fold(3)
+    for copy in f_rest:
+        copy.wait_recv()
+    for h in range(2):
+        at = pl.ds(8 * h, 8)
+        f_mine[:, at] = total[:, y, at] + f_ins[0, h] + f_ins[1, h]
+    f_swap = far.start(f_mine.at[1 - zh], f_got, device(rep, zl, x, 1 - zh, y))
+    for copy in x_rest:
+        copy.wait_recv()
+    for h in range(2):
+        at = pl.ds(2 * h, 2)
+        w1[:, at] = acc[:, x, at] + x_ins[0, h] + x_ins[1, h]
+
+    def y_part(ny, h):
+        return w1.at[:, ny, pl.ds(40 * h, 40)]
+
+    y_first = ring_first(far, y, y_part, y_hops, on_y)
+    y_rest = ring_rest(far, y, y_part, y_first, y_hops, y_ins, on_y)
+    for copy in y_rest:
+        copy.wait_recv()
+    for h in range(2):
+        at = pl.ds(40 * h, 40)
+        w2[:, at] = w1[:, y, at] + y_ins[0, h] + y_ins[1, h]
+    z_made = [far.start(w2.at[a], z_got.at[i], device(rep, a, x, b, y)) for i, (a, b) in enumerate(zs)]
+    f_swap.wait_recv()
+    out[...] = f_mine[zh] + f_got[...]
+    w3 = w2[zl]
+    for i, copy in enumerate(z_made):
+        copy.wait_recv()
+        w3 = w3 + z_got[i]
+    slot = rep * 4 + y
+    packed[slot] = w3
+    ag_made = [
+        far.start(packed.at[slot], packed.at[slot], device(a, zl, x, zh, b)) for a, b in ags
+    ]
+    for copy in ag_made:
+        copy.wait_recv()
+    base, step = 0, packed.shape[1]
+    for o in (o0, o1, o2, o3, o4):
+        per = o.shape[0]
+        for j in range(o.shape[1] // 128):
+            done = 0
+            while done < per:
+                blk, off = (base + done) // step, (base + done) % step
+                n = min(per - done, step - off)
+                o[done : done + n, j * 128 : (j + 1) * 128] = packed[blk, off : off + n, :]
+                done += n
+            base += per
+    far.drain()
+
+
+def reduce(total, wg, weights, owners):
+    feat = total.shape[1]
+    chans = wg.shape[2]
+    total = total.reshape(2, 4, 16, feat)
+    wg = wg.reshape(4, 4, 8, PACK // 8, chans)
+    q = PACK // 8
+    vm = pl.BlockSpec(memory_space=pltpu.VMEM)
+    count = 4 + 6 + 6 + 1 + 6 + 7 + 7
+    outs = pl.pallas_call(
+        reduce_kernel,
+        out_shape=(
+            jax.ShapeDtypeStruct((16, feat), F32),
+            *[jax.ShapeDtypeStruct((w.shape[0] // owners, w.shape[1]), F32) for w in weights],
+        ),
+        in_specs=[vm, vm],
+        out_specs=(vm,) * 6,
+        scratch_shapes=[
+            pltpu.VMEM((2, 2, 8, feat), F32),
+            pltpu.VMEM((2, 2, 2, 8, feat), F32),
+            pltpu.VMEM((2, 16, feat), F32),
+            pltpu.VMEM((16, feat), F32),
+            pltpu.VMEM((4, 4, 4, q, chans), F32),
+            pltpu.VMEM((4, 4, 4, q, chans), F32),
+            pltpu.VMEM((2, 4, 2, q, chans), F32),
+            pltpu.VMEM((2, 2, 4, 2, q, chans), F32),
+            pltpu.VMEM((4, 4, q, chans), F32),
+            pltpu.VMEM((2, 4, q // 2, chans), F32),
+            pltpu.VMEM((2, 2, 4, q // 2, chans), F32),
+            pltpu.VMEM((4, q, chans), F32),
+            pltpu.VMEM((7, q, chans), F32),
+            pltpu.VMEM((8, q, chans), F32),
+            pltpu.SemaphoreType.DMA((count,)),
+            pltpu.SemaphoreType.DMA((count,)),
+        ],
+        compiler_params=pltpu.CompilerParams(
+            collective_id=1, has_side_effects=True, vmem_limit_bytes=48 * 2**20
+        ),
+        name="gather_sums",
+    )(total, wg)
     return outs
 
 
 def local(src_feats, tgt_cotangent, rotation, edge_src, edge_tgt, edge_count, *weights):
-    chans = weights[0].shape[0] // 5
-    owners = lax.axis_size("src")
-    xb = lax.all_gather(src_feats[0], "tgt", axis=0, tiled=True)
-    gb = lax.all_gather(tgt_cotangent[0], "src", axis=0, tiled=True)
+    owners, n_tgt = lax.axis_size("src"), lax.axis_size("tgt")
+    feat = src_feats.shape[2]
+    xb, gb = gather(src_feats[0], tgt_cotangent[0], owners, n_tgt)
     total, wg = compute(
-        xb, gb, rotation[0, 0, 0], edge_src[0, 0], edge_tgt[0, 0], edge_count[0, 0], weights, owners
+        xb.reshape(-1, feat), gb.reshape(-1, feat), rotation[0, 0, 0], edge_src[0, 0], edge_tgt[0, 0],
+        edge_count[0, 0], weights, owners,
     )
-    part = lax.psum_scatter(wg, "src", scatter_dimension=0, tiled=True)[0]
-    grad_feats = lax.psum_scatter(total[None], "tgt", scatter_dimension=1, tiled=True)
-    packed = lax.psum(part, ("rep", "tgt"))
-    return (grad_feats, *unpack(packed, weights, owners, chans))
+    grad_feats, *grads = reduce(total, wg, weights, owners)
+    return (grad_feats[None], *grads)
 
 
 def solution(mesh):

time: 591 us -> 162 us (0.27)
  waiting for transfers between devices: 527 us -> 0 us
  Pallas kernels: 42.7 us -> 149 us
  between operations: 14.4 us -> 1.31 us
    psum x1 -> x0, waiting for transfers between devices: 190 us -> none  [local(): packed = lax.psum(part, ('rep', 'tgt'))]
    all_gather x2 -> x0, waiting for transfers between devices: 148 us -> none  [the longest x1 77.5 us: local(): gb = lax.all_gather(tgt_cotangent[0], 'src', axis=0, tiled=True)]
    pallas_call x0 -> x2, Pallas kernels: none -> 106 us  [the longest x1 61.5 us: reduce(): pl.pallas_call(reduce_kernel, out_shape=(jax.ShapeDtypeStruct((16, feat),...]
    unnamed x6 -> x0, waiting for transfers between devices: 96.6 us -> none
    reduce_scatter x1 -> x0, waiting for transfers between devices: 92.5 us -> none  [local(): lax.psum_scatter(total[None], 'tgt', scatter_dimension=1, tiled=True)]
    unnamed x2 -> x17, local copies, waits for them, and re-layouts: 2.27 us -> 11.6 us
  transfers between devices with their start and end apart: 5 -> 0, of which waited for: 5 -> 0; matrix products, arithmetic and copies ran while one was open for 1% -> 0% of each run, Pallas kernels for 0% -> 0%
where the time goes in v2:
time: 162 us; the launch traced here: 161 us
  Pallas kernels  149 us (92%)
  local copies, waits for them, and re-layouts  11.6 us (7%)
    pallas_call x1, Pallas kernels, reduce(): pl.pallas_call(reduce_kernel, out_shape=(jax.ShapeDtypeStruct((16, feat),...  61.5 us
    pallas_call x1, Pallas kernels, gather(): pl.pallas_call(gather_kernel, out_shape=(jax.ShapeDtypeStruct((n_tgt, row...  44.3 us
    pallas_call x1, Pallas kernels, compute(): pl.pallas_call(compute_kernel, out_shape=(jax.ShapeDtypeStruct((src_blk,...  42.7 us
    unnamed x17, local copies, waits for them, and re-layouts  11.6 us

profile of v2, /device:TPU:1, one launch (start us, length us, event | category | flops | bytes accessed | tf_op | source)
XLA Modules:
  0.0 161.5 jit_solution(3803825546138181296)
XLA Ops:
  1.3 1.6 copy.19
  2.9 0.0 copy-start.3
  2.9 0.9 copy-done.3
  3.8 0.0 copy-start.4
  3.8 0.9 copy-done.4
  4.7 44.3 %spread.1 = (f32[8,16,3200]{2,1,0:T(8,128)S(1)}, f32[16,16,3200]{2,1,0:T(8,128)S(1)}) custom-call(f32[16,3200]{1,0:T(8,128)S(1)} %bitcast.17, f32[16,3200]{1,0:T(8,128)S(1)} %bitcast.18), custom_call_target="tpu_custom_call" | custom-call | tf_op jit(solution)/shard_map/spread/pallas_call | solution.py:356
  49.1 0.0 copy-start
  49.1 1.7 %copy-done = f32[16,16,3200]{2,1,0:T(8,128)} copy-done((f32[16,16,3200]{2,1,0:T(8,128)}, f32[16,16,3200]{2,1,0:T(8,128)S(1)}, u32[]{:S(2)}) %copy-start) | copy-done | bytes 3276824
  50.7 0.0 copy-start.2
  50.7 1.2 copy-done.2
  52.0 42.7 %tile.1 = (f32[128,3200]{1,0:T(8,128)}, f32[16,640,128]{2,1,0:T(8,128)}) custom-call(s32[1]{0:T(128)} %bitcast.13.cnt_ref, f32[128,3200]{1,0:T(8,128)} %bitcast.16, f32[256,3200]{1,0:T(8,128)} %bitcast.14, f32[115,384]{1,0:T(8,128)} %bitcast.21, s32[1,384]{1,0:T(1,128)} %bitcast.22, s32[1,384]{1,0:T(1,128)} %bitcast.23, f32[640,640]{1,0:T(8,128)} %w0_ref.1, ...), custom_call_target="tpu_custom_call" | custom-call | tf_op jit(solution)/shard_map/tile/pallas_call | solution.py:222
  94.7 0.0 copy-start.1
  94.7 1.4 copy-done.1
  96.1 61.5 %gather_sums.1 = (f32[16,3200]{1,0:T(8,128)S(1)}, f32[40,640]{1,0:T(8,128)S(1)}, f32[32,512]{1,0:T(8,128)S(1)}, f32[32,512]{1,0:T(8,128)S(1)}, f32[24,384]{1,0:T(8,128)S(1)}, /*index=5*/f32[24,384]{1,0:T(8,128)S(1)}) custom-call(f32[2,4,16,3200]{3,2,1,0:T(8,128)S(1)} %bitcast.15, f32[4,4,8,80,128]{4,3,2,1,0:T(8,128)} %bitcast.20), custom_call_target="tpu_custom_call" | custom-call | tf_op jit(solution)/shard_map/gather_sums/pallas_call | solution.py:503
  157.6 0.7 copy.27
  158.3 0.6 copy.28
  159.0 0.6 copy.29
  159.6 0.6 copy.30
  160.2 0.6 copy.31
  160.8 0.6 copy.32
Async XLA Ops:
  2.9 0.9 copy-start.3
  3.8 0.9 copy-start.4
  49.1 1.7 %copy-start = (f32[16,16,3200]{2,1,0:T(8,128)}, f32[16,16,3200]{2,1,0:T(8,128)S(1)}, u32[]{:S(2)}) copy-start(f32[16,16,3200]{2,1,0:T(8,128)S(1)} %get-tuple-element.17) | copy-start | bytes 9830404
  50.7 1.2 copy-start.2
  94.7 1.4 copy-start.1

commit v3 on v1

v3 whole, which is shorter than its diff:
```python
import jax
import jax.numpy as jnp
from jax import lax
from jax.experimental import pallas as pl
from jax.experimental.pallas import tpu as pltpu
from jax.sharding import PartitionSpec as P

OFFSETS = (0, 1, 10, 35, 70)
F32, BF16 = jnp.float32, jnp.bfloat16
MESH = pl.DeviceIdType.MESH
PACK = 640
NT = (((1,), (1,)), ((), ()))
NN = (((1,), (0,)), ((), ()))


def mm(a, b, dims):
    return lax.dot_general(a, b, dims, preferred_element_type=F32)


def split(a):
    hi = a.astype(BF16)
    return hi, (a - hi.astype(F32)).astype(BF16)


def onehot(ids, live, atoms):
    rows = lax.broadcasted_iota(jnp.int32, (atoms, ids.shape[1]), 0)
    return jnp.where((rows == ids) & live, 1.0, 0.0).astype(BF16)


def place():
    rep, src, tgt = lax.axis_index("rep"), lax.axis_index("src"), lax.axis_index("tgt")
    return rep, src // 4, src % 4, tgt // 4, tgt % 4


def device(rep, zl, x, zh, y):
    return (rep, zl * 4 + x, zh * 4 + y)


def pair(i, d):
    return (i + 1 - 2 * (i % 2), (i + 2) % 4, 3 - i)[d - 1]


class Copies:
    def __init__(self, send, recv):
        self.send, self.recv, self.made = send, recv, []

    def start(self, src, dst, to):
        n = len(self.made)
        copy = pltpu.make_async_remote_copy(
            src_ref=src, dst_ref=dst, send_sem=self.send.at[n], recv_sem=self.recv.at[n],
            device_id=to, device_id_type=MESH,
        )
        copy.start()
        self.made.append(copy)
        return copy

    def drain(self):
        for copy in self.made:
            copy.wait_send()


def greet(peers):
    barrier = pltpu.get_barrier_semaphore()
    for peer in peers:
        pl.semaphore_signal(barrier, inc=1, device_id=peer, device_id_type=MESH)
    pl.semaphore_wait(barrier, len(peers))


def ring_first(far, me, part, hops, to):
    right, left, opp = (me + 1) % 4, (me + 3) % 4, (me + 2) % 4
    return (
        far.start(part(opp, 0), hops.at[0], to(right)),
        far.start(part(opp, 1), hops.at[1], to(left)),
    )


def ring_own(far, me, part, ins, to):
    right, left = (me + 1) % 4, (me + 3) % 4
    return [
        far.start(part(right, 1), ins.at[0, 1], to(right)),
        far.start(part(left, 0), ins.at[1, 0], to(left)),
    ]


def ring_rest(far, me, part, firsts, hops, ins, to):
    right, left = (me + 1) % 4, (me + 3) % 4
    made = []
    firsts[0].wait_recv()
    hops[0] = hops[0] + part(right, 0)[...]
    made.append(far.start(hops.at[0], ins.at[0, 0], to(right)))
    firsts[1].wait_recv()
    hops[1] = hops[1] + part(left, 1)[...]
    made.append(far.start(hops.at[1], ins.at[1, 1], to(left)))
    return made


def pick(block_ref, hot_ref, out_ref, first, width, count):
    def one(i, carry):
        at = pl.multiple_of(first + i * width, 128)
        block = block_ref[:, :, pl.ds(at, width)]
        hi, lo = split(block.reshape(-1, width).T)
        out_ref[pl.ds(at, width), :] = mm(jnp.concatenate([hi, lo], 1), hot_ref[...], NN)
        return carry

    lax.fori_loop(0, count, one, 0)


def rotate(rows_ref, rot_ref, put, chans, cap, levels):
    steps, lanes = 16, 128
    tiles = cap // lanes

    def one(i, carry):
        ch = pl.multiple_of((i // tiles) * steps, steps)
        ln = pl.multiple_of((i % tiles) * lanes, lanes)
        for level in levels:
            q, cols = min(level, 2), 2 * level + 1
            xs = [
                rows_ref[pl.ds((level * level + c) * chans + ch, steps), pl.ds(ln, lanes)]
                for c in range(cols)
            ]
            for r in range(2 * q + 1):
                acc = None
                for c in range(cols):
                    o = OFFSETS[level] + r * cols + c
                    term = rot_ref[o, :, pl.ds(ln, lanes)] * xs[c]
                    acc = term if acc is None else acc + term
                m = r - q
                put(abs(m), m < 0, level - abs(m), ch, ln, acc)
        return carry

    lax.fori_loop(0, (chans // steps) * tiles, one, 0)


def pieces(first, count, step):
    done = 0
    while done < count:
        blk, off = (first + done) // step, (first + done) % step
        n = min(count - done, step - off)
        yield blk, off, done, n
        done += n


def tile_kernel(
    cnt_ref, es_ref, et_ref, x_in, g_in, rot_in, w0_in, w1r_in, w1i_in, w2r_in, w2i_in,
    out, packed,
    rot_ref, wf0, wf1r, wf1i, wf2r, wf2i, wh0, wh1r, wh1i, wh2r, wh2i,
    x_ref, g_ref, hs_ref, ht_ref, hs2_ref, rows_ref,
    z0_ref, z1_ref, z2_ref, u0_ref, u1_ref, u2_ref, v1_ref, v2_ref, term_ref,
    total, wg, f_hops, f_ins, f_mine, f_got, halves, x_hops, x_ins, w1, y_hops, y_ins, w2, z_got,
    send, recv, own,
):
    rep, zl, x, zh, y = place()
    cap, chans, feat = es_ref.shape[1], 128, x_in.shape[1]
    src_blk, tgt_blk = hs_ref.shape[0] // 2, ht_ref.shape[0] // 2
    owned = [
        pltpu.make_async_copy(a, b, own.at[i])
        for i, (a, b) in enumerate(
            ((w0_in, wf0), (w1r_in, wf1r), (w1i_in, wf1i), (w2r_in, wf2r), (w2i_in, wf2i), (rot_in, rot_ref))
        )
    ]

    right, left = (x + 1) % 4, (x + 3) % 4
    up, down = (y + 1) % 4, (y + 3) % 4
    zs = [(pair(zl, d) if d else zl, (1 - zh) if far_z else zh) for far_z in (0, 1) for d in range(4)][1:]
    ags = [((rep + dr) % 2, (y + dy) % 4) for dr in (0, 1) for dy in range(4)][1:]
    lines = [pair(zl, d) for d in (1, 2, 3)]
    across, other = device(rep, zl, x, 1 - zh, y), device(1 - rep, zl, x, zh, y)

    def on_x(nx):
        return device(rep, zl, nx, zh, y)

    def on_y(ny):
        return device(rep, zl, x, zh, ny)

    def on_z(nz):
        return device(rep, nz, x, zh, y)

    greet(
        [on_x(left), on_x(right)]
        + [device(rep, a, x, b, y) for a, b in zs]
        + [device(a, zl, x, zh, b) for a, b in ags]
    )
    far = Copies(send, recv)

    mine_g, mine_x = zl * 4 + x, zh * 4 + y
    parts = (pl.ds(0, 16 * chans), pl.ds(16 * chans, 9 * chans))
    whole = pl.ds(0, feat)

    def both(src, slot, at, out_ref, to, one, two):
        dst = out_ref.at[slot, :, at]
        return far.start(src, dst, to(one)), far.start(src, dst, to(two))

    def relay(copies, out_ref, at, slots, to, one, two):
        copies[0].wait_recv()
        ref = out_ref.at[slots[0], :8, at]
        a = far.start(ref, ref, to(one))
        copies[1].wait_recv()
        ref = out_ref.at[slots[1], 8:, at]
        return a, far.start(ref, ref, to(two))

    z_go = [None, None]
    xs, ends_g, ends_x, ys = ([], []), ([], []), [], []

    def z_start(p):
        at = parts[p]
        z_go[p] = [far.start(g_in.at[:, at], g_ref.at[mine_g, :, at], on_z(n)) for n in lines]

    z_start(0)
    hop = far.start(x_in, x_ref.at[mine_x], across)
    xs[0].append(both(g_in.at[:, parts[0]], mine_g, parts[0], g_ref, on_x, right, left))
    ys.append(both(x_in, mine_x, whole, x_ref, on_y, up, down))
    z_start(1)
    xs[1].append(both(g_in.at[:, parts[1]], mine_g, parts[1], g_ref, on_x, right, left))
    owned.append(pltpu.make_async_copy(g_in, g_ref.at[mine_g], own.at[6]))
    owned.append(pltpu.make_async_copy(x_in, x_ref.at[mine_x], own.at[7]))
    for copy in owned:
        copy.start()
    order = [zl, *lines]

    def x_step(p, j):
        z_go[p][j - 1].wait_recv()
        slot = order[j] * 4 + x
        xs[p].append(both(g_ref.at[slot, :, parts[p]], slot, parts[p], g_ref, on_x, right, left))

    def x_relay(p, j):
        slots = (order[j] * 4 + left, order[j] * 4 + right)
        ends_g[p].extend(relay(xs[p][j], g_ref, parts[p], slots, on_x, right, left))

    def y_relay(j):
        at = (zh, 1 - zh)[j] * 4
        ends_x.extend(relay(ys[j], x_ref, whole, (at + down, at + up), on_y, up, down))

    live = lax.broadcasted_iota(jnp.int32, (1, cap), 1) < cnt_ref[0]
    hot = onehot(es_ref[...], live, src_blk)
    hs_ref[:src_blk, :] = hot
    hs_ref[src_blk:, :] = hot
    hs2_ref[:, :cap] = hot
    hs2_ref[:, cap:] = hot
    hot = onehot(et_ref[...], live, tgt_blk)
    ht_ref[:tgt_blk, :] = hot
    ht_ref[tgt_blk:, :] = hot
    for copy in owned:
        copy.wait()
    for src, dst in ((wf0, wh0), (wf1r, wh1r), (wf1i, wh1i), (wf2r, wh2r), (wf2i, wh2i)):
        def cut(i, carry, src=src, dst=dst):
            at = pl.ds(pl.multiple_of(i * 128, 128), 128)
            dst[0, at, :], dst[1, at, :] = split(src[at, :])
            return carry

        lax.fori_loop(0, src.shape[0] // 128, cut, 0)

    x_step(0, 1)
    x_relay(0, 0)
    y_relay(0)
    x_step(0, 2)
    x_relay(0, 1)
    hop.wait_recv()
    slot = (1 - zh) * 4 + y
    ys.append(both(x_ref.at[slot], slot, whole, x_ref, on_y, up, down))
    x_step(0, 3)
    x_relay(0, 2)
    y_relay(1)
    x_step(1, 1)
    x_relay(0, 3)
    x_relay(1, 0)
    x_step(1, 2)
    for copy in ends_x:
        copy.wait_recv()

    zrefs = (z0_ref, z1_ref, z2_ref)

    def put_z(order, neg, k, ch, ln, val):
        hi, lo = split(val)
        rows = pl.ds(k * chans + ch, 16)
        at = pl.ds(ln + (cap if neg else 0), 128)
        zrefs[order][0, rows, at] = hi
        zrefs[order][1, rows, at] = lo

    pick(x_ref, hs_ref, rows_ref, 0, 5 * chans, 5)
    x_relay(1, 1)
    x_step(1, 3)
    x_relay(1, 2)
    rotate(rows_ref, rot_ref, put_z, chans, cap, range(5))
    x_relay(1, 3)

    urefs = (u0_ref, u1_ref, u2_ref)
    vrefs = (None, v1_ref, v2_ref)

    def put_u(order, neg, k, ch, ln, val):
        hi, lo = split(val)
        rows = pl.ds(k * chans + ch, 16)
        at = pl.ds(ln + (cap if neg else 0), 128)
        urefs[order][0, rows, at] = hi
        urefs[order][1, rows, at] = lo
        if order:
            at = pl.ds(ln + (0 if neg else cap), 128)
            vrefs[order][0, rows, at] = hi if neg else -hi
            vrefs[order][1, rows, at] = lo if neg else -lo

    for copy in ends_g[0]:
        copy.wait_recv()
    pick(g_ref, ht_ref, rows_ref, 0, 4 * chans, 4)
    rotate(rows_ref, rot_ref, put_u, chans, cap, range(4))
    for copy in ends_g[1]:
        copy.wait_recv()
    pick(g_ref, ht_ref, rows_ref, 16 * chans, 3 * chans, 3)
    rotate(rows_ref, rot_ref, put_u, chans, cap, (4,))

    def grad(z, u, at, count):
        zhi, zlo = z[0, pl.ds(at, count), :], z[1, pl.ds(at, count), :]
        return mm(zhi, u[0], NT) + mm(zhi, u[1], NT) + mm(zlo, u[0], NT)

    quarter = wg.shape[3]
    xorder = [(x + 2) % 4, right, left, x]
    swaps = []
    for h in range(2):
        base = 0
        for zr, ur, cols in (
            (z0_ref, u0_ref, 5), (z1_ref, u1_ref, 4), (z1_ref, v1_ref, 4), (z2_ref, u2_ref, 3), (z2_ref, v2_ref, 3),
        ):
            per = cols * chans // 16
            res = grad(zr, ur, h * 8 * per, 8 * per)
            for s in range(8):
                for j in range(cols):
                    for blk, off, done, n in pieces(base + j * per, per, quarter):
                        wg[2 * h + s // 4, s % 4, blk, off : off + n, :] = res[
                            s * per + done : s * per + done + n, j * chans : (j + 1) * chans
                        ]
            base += cols * per
        for blk, off, done, n in pieces(base, 8 * quarter - base, quarter):
            wg[2 * h : 2 * h + 2, :, blk, off : off + n, :] = jnp.zeros((2, 4, n, chans), F32)
        for nx in xorder:
            zz = pl.ds(2 * h, 2)
            swaps.append(far.start(wg.at[zz, nx, pl.ds(4 * (1 - rep), 4)], halves.at[zz, nx], other))

    def three(w, u):
        return mm(w[0], u[0], NN) + mm(w[0], u[1], NN) + mm(w[1], u[0], NN)

    firsts = (0, 5 * chans, 13 * chans)

    def keep(order, res):
        rows = res.shape[0]
        rows_ref[firsts[order] : firsts[order] + rows, :] = res[:, :cap]
        if order:
            rows_ref[firsts[order] + rows : firsts[order] + 2 * rows, :] = res[:, cap:]

    def fold(i):
        swaps[i].wait_recv()
        swaps[4 + i].wait_recv()
        nx = xorder[i]
        halves[:, nx] = wg[:, nx, pl.ds(4 * rep, 4)] + halves[:, nx]

    def x_part(nx, h):
        return halves.at[:, nx, pl.ds(2 * h, 2)]

    keep(0, three(wh0, u0_ref))
    keep(2, three(wh2r, u2_ref) + three(wh2i, v2_ref))
    fold(0)
    x_first = ring_first(far, x, x_part, x_hops, on_x)
    fold(1)
    fold(2)
    x_rest = ring_own(far, x, x_part, x_ins, on_x)
    fold(3)
    keep(1, three(wh1r, u1_ref) + three(wh1i, v1_ref))
    x_rest += ring_rest(far, x, x_part, x_first, x_hops, x_ins, on_x)

    tiles = cap // 128

    def back(i, carry):
        ch = pl.multiple_of((i // tiles) * 16, 16)
        ln = pl.multiple_of((i % tiles) * 128, 128)
        for level in range(5):
            q, cols = min(level, 2), 2 * level + 1
            ds = []
            for r in range(2 * q + 1):
                m = r - q
                k = level - abs(m) + (((5 - abs(m)) if m < 0 else 0))
                ds.append(rows_ref[pl.ds(firsts[abs(m)] + k * chans + ch, 16), pl.ds(ln, 128)])
            for c in range(cols):
                acc = None
                for r in range(2 * q + 1):
                    o = OFFSETS[level] + r * cols + c
                    term = rot_ref[o, :, pl.ds(ln, 128)] * ds[r]
                    acc = term if acc is None else acc + term
                hi, lo = split(acc)
                rows = pl.ds((level * level + c) * chans + ch, 16)
                term_ref[rows, pl.ds(ln, 128)] = hi
                term_ref[rows, pl.ds(ln + cap, 128)] = lo
        return carry

    lax.fori_loop(0, (chans // 16) * tiles, back, 0)

    def scatter(c, carry):
        at = pl.multiple_of(c * 5 * chans, chans)
        res = mm(hs2_ref[...], term_ref[pl.ds(at, 5 * chans), :], NT)
        total[:, :, :, pl.ds(at, 5 * chans)] = res.reshape(2, 4, 16, 5 * chans)
        return carry

    lax.fori_loop(0, 5, scatter, 0)

    def f_part(ny, h):
        return total.at[:, ny, pl.ds(8 * h, 8)]

    f_first = ring_first(far, y, f_part, f_hops, on_y)
    f_rest = ring_own(far, y, f_part, f_ins, on_y)
    for copy in x_rest:
        copy.wait_recv()
    for h in range(2):
        at = pl.ds(2 * h, 2)
        w1[:, at] = halves[:, x, at] + x_ins[0, h] + x_ins[1, h]

    def y_part(ny, h):
        return w1.at[:, ny, pl.ds(40 * h, 40)]

    y_first = ring_first(far, y, y_part, y_hops, on_y)
    f_rest += ring_rest(far, y, f_part, f_first, f_hops, f_ins, on_y)
    y_rest = ring_own(far, y, y_part, y_ins, on_y)
    y_rest += ring_rest(far, y, y_part, y_first, y_hops, y_ins, on_y)
    for copy in f_rest:
        copy.wait_recv()
    for h in range(2):
        at = pl.ds(8 * h, 8)
        f_mine[:, at] = total[:, y, at] + f_ins[0, h] + f_ins[1, h]
    f_swap = far.start(f_mine.at[1 - zh], f_got, across)
    for copy in y_rest:
        copy.wait_recv()
    for h in range(2):
        at = pl.ds(40 * h, 40)
        w2[:, at] = w1[:, y, at] + y_ins[0, h] + y_ins[1, h]
    z_made = [far.start(w2.at[a], z_got.at[i], device(rep, a, x, b, y)) for i, (a, b) in enumerate(zs)]
    w3 = w2[zl]
    for i, copy in enumerate(z_made):
        copy.wait_recv()
        w3 = w3 + z_got[i]
    slot = rep * 4 + y
    packed[slot] = w3
    ag_made = [
        far.start(packed.at[slot], packed.at[slot], device(a, zl, x, zh, b)) for a, b in ags
    ]
    f_swap.wait_recv()
    out[...] = f_mine[zh] + f_got[...]
    for copy in ag_made:
        copy.wait_recv()
    far.drain()


def finish_kernel(feats, packed, out, o0, o1, o2, o3, o4):
    out[...] = feats[...]
    base = 0
    for o in (o0, o1, o2, o3, o4):
        per = o.shape[0]
        for j in range(o.shape[1] // 128):
            for blk, off, done, n in pieces(base, per, packed.shape[1]):
                o[done : done + n, j * 128 : (j + 1) * 128] = packed[blk, off : off + n, :]
            base += per


def run(src_feats, tgt_cotangent, wig, es, et, cnt, weights, owners, n_tgt):
    cap = es.shape[1]
    chans = 128
    rows, feat = src_feats.shape
    src_blk, tgt_blk = n_tgt * rows, owners * rows
    q = PACK // 8
    vm = pl.BlockSpec(memory_space=pltpu.VMEM)
    anywhere = pl.BlockSpec(memory_space=pl.ANY)
    dims = [w.shape[0] for w in weights]
    count = 2 * 19 + 9 + 8 + 6 + 6 + 1 + 6 + 7 + 7
    feats, packed = pl.pallas_call(
        tile_kernel,
        out_shape=(
            jax.ShapeDtypeStruct((rows, feat), F32),
            jax.ShapeDtypeStruct((8, q, chans), F32),
        ),
        in_specs=[pl.BlockSpec(memory_space=pltpu.SMEM), vm, vm] + [anywhere] * 8,
        out_specs=(vm, vm),
        scratch_shapes=[
            pltpu.VMEM(wig.shape, F32),
            *[pltpu.VMEM((d, d), F32) for d in dims],
            *[pltpu.VMEM((2, d, d), BF16) for d in dims],
            pltpu.VMEM((n_tgt, rows, feat), F32),
            pltpu.VMEM((owners, rows, feat), F32),
            pltpu.VMEM((2 * src_blk, cap), BF16),
            pltpu.VMEM((2 * tgt_blk, cap), BF16),
            pltpu.VMEM((src_blk, 2 * cap), BF16),
            pltpu.VMEM((feat, cap), F32),
            pltpu.VMEM((2, dims[0], cap), BF16),
            pltpu.VMEM((2, dims[1], 2 * cap), BF16),
            pltpu.VMEM((2, dims[3], 2 * cap), BF16),
            pltpu.VMEM((2, dims[0], cap), BF16),
            pltpu.VMEM((2, dims[1], 2 * cap), BF16),
            pltpu.VMEM((2, dims[3], 2 * cap), BF16),
            pltpu.VMEM((2, dims[1], 2 * cap), BF16),
            pltpu.VMEM((2, dims[3], 2 * cap), BF16),
            pltpu.VMEM((feat, 2 * cap), BF16),
            pltpu.VMEM((2, 4, rows, feat), F32),
            pltpu.VMEM((4, 4, 8, q, chans), F32),
            pltpu.VMEM((2, 2, 8, feat), F32),
            pltpu.VMEM((2, 2, 2, 8, feat), F32),
            pltpu.VMEM((2, rows, feat), F32),
            pltpu.VMEM((rows, feat), F32),
            pltpu.VMEM((4, 4, 4, q, chans), F32),
            pltpu.VMEM((2, 4, 2, q, chans), F32),
            pltpu.VMEM((2, 2, 4, 2, q, chans), F32),
            pltpu.VMEM((4, 4, q, chans), F32),
            pltpu.VMEM((2, 4, q // 2, chans), F32),
            pltpu.VMEM((2, 2, 4, q // 2, chans), F32),
            pltpu.VMEM((4, q, chans), F32),
            pltpu.VMEM((7, q, chans), F32),
            pltpu.SemaphoreType.DMA((count,)),
            pltpu.SemaphoreType.DMA((count,)),
            pltpu.SemaphoreType.DMA((8,)),
        ],
        compiler_params=pltpu.CompilerParams(
            collective_id=0, has_side_effects=True, vmem_limit_bytes=62 * 2**20
        ),
        name="tile",
    )(cnt, es, et, src_feats, tgt_cotangent, wig, *weights)
    return pl.pallas_call(
        finish_kernel,
        out_shape=(
            jax.ShapeDtypeStruct((rows, feat), F32),
            *[jax.ShapeDtypeStruct((d // owners, d), F32) for d in dims],
        ),
        in_specs=[vm, vm],
        out_specs=(vm,) * 6,
        name="finish",
    )(feats, packed)


def local(src_feats, tgt_cotangent, rotation, edge_src, edge_tgt, edge_count, *weights):
    wig = rotation.transpose(0, 1, 3, 2, 4)[0, 0]
    grad_feats, *grads = run(
        src_feats[0], tgt_cotangent[0], wig, edge_src[0, 0], edge_tgt[0, 0], edge_count[0, 0], weights,
        lax.axis_size("src"), lax.axis_size("tgt"),
    )
    return (grad_feats[None], *grads)


def solution(mesh):
    placed = (
        P("rep", ("src", "tgt"), None),
        P("rep", ("tgt", "src"), None),
        P("rep", "src", "tgt", None, None),
        P("rep", "src", "tgt", None),
        P("rep", "src", "tgt", None),
        P("rep", "src", "tgt"),
        P(), P(), P(), P(), P(),
    )
    return jax.shard_map(
        local,
        mesh=mesh,
        in_specs=placed,
        out_specs=(P("rep", ("src", "tgt"), None), *[P("src", None)] * 5),
        check_vma=False,
    )
```

time: 591 us -> 125 us (0.21)
  waiting for transfers between devices: 527 us -> 0 us
  Pallas kernels: 42.7 us -> 123 us
  between operations: 14.4 us -> 1.29 us
  local copies, waits for them, and re-layouts: 6.2 us -> 0 us
    psum x1 -> x0, waiting for transfers between devices: 190 us -> none  [local(): packed = lax.psum(part, ('rep', 'tgt'))]
    all_gather x2 -> x0, waiting for transfers between devices: 148 us -> none  [the longest x1 77.5 us: local(): gb = lax.all_gather(tgt_cotangent[0], 'src', axis=0, tiled=True)]
    unnamed x6 -> x0, waiting for transfers between devices: 96.6 us -> none
    reduce_scatter x1 -> x0, waiting for transfers between devices: 92.5 us -> none  [local(): lax.psum_scatter(total[None], 'tgt', scatter_dimension=1, tiled=True)]
    pallas_call x1 -> x2, Pallas kernels: 42.7 us -> 123 us  [the longest x1 121 us: run(): pl.pallas_call(tile_kernel, out_shape=(jax.ShapeDtypeStruct((rows, feat),...]
  transfers between devices with their start and end apart: 5 -> 0, of which waited for: 5 -> 0; matrix products, arithmetic and copies ran while one was open for 1% -> 0% of each run, Pallas kernels for 0% -> 0%
where the time goes in v3:
time: 125 us; the launch traced here: 124 us
  Pallas kernels  123 us (98%)
  between operations  1.29 us (1%)
    pallas_call x1, Pallas kernels, run(): pl.pallas_call(tile_kernel, out_shape=(jax.ShapeDtypeStruct((rows, feat),...  121 us

profile of v3, /device:TPU:1, one launch (start us, length us, event | category | flops | bytes accessed | tf_op | source)
XLA Modules:
  0.0 124.4 jit_solution(5716914589096226035)
XLA Ops:
  1.3 121.2 %tile.1 = (f32[16,3200]{1,0:T(8,128)}, f32[8,80,128]{2,1,0:T(8,128)}) custom-call(s32[1]{0:T(128)} %bitcast.7.cnt_ref, s32[1,384]{1,0:T(1,128)} %bitcast.11, s32[1,384]{1,0:T(1,128)} %bitcast.12, f32[16,3200]{1,0:T(8,128)} %bitcast.8, f32[16,3200]{1,0:T(8,128)} %bitcast.9, f32[115,1,384]{2,1,0:T(1,128)} %bitcast.10, f32[640,640]{1,0:T(8,128)} %w0_in.1, ...), custom_call_target="tpu_custom_call" | custom-call | tf_op jit(solution)/shard_map/tile/pallas_call | solution.py:468
  122.5 1.9 %finish.1 = (f32[16,3200]{1,0:T(8,128)}, f32[40,640]{1,0:T(8,128)}, f32[32,512]{1,0:T(8,128)}, f32[32,512]{1,0:T(8,128)}, f32[24,384]{1,0:T(8,128)}, /*index=5*/f32[24,384]{1,0:T(8,128)}) custom-call(f32[16,3200]{1,0:T(8,128)} %get-tuple-element.14.feats, f32[8,80,128]{2,1,0:T(8,128)} %get-tuple-element.15.packed), custom_call_target="tpu_custom_call" | custom-call | tf_op jit(solution)/shard_map/finish/pallas_call | solution.py:518

commit v4 on v3

--- a/solution.py
+++ b/solution.py
@@ -1,3 +1,5 @@
+import functools
+
 import jax
 import jax.numpy as jnp
 from jax import lax
@@ -146,8 +148,9 @@
     rot_ref, wf0, wf1r, wf1i, wf2r, wf2i, wh0, wh1r, wh1i, wh2r, wh2i,
     x_ref, g_ref, hs_ref, ht_ref, hs2_ref, rows_ref,
     z0_ref, z1_ref, z2_ref, u0_ref, u1_ref, u2_ref, v1_ref, v2_ref, term_ref,
-    total, wg, f_hops, f_ins, f_mine, f_got, halves, x_hops, x_ins, w1, y_hops, y_ins, w2, z_got,
-    send, recv, own,
+    total, wg, f_hops, f_ins, f_mine, f_got, halves, a_hops, a_ins, b_hops, b_ins,
+    wa, wb, a2_hops, a2_ins, b2_hops, b2_ins, w2, z_got,
+    send, recv, line_send, line_recv, own,
 ):
     rep, zl, x, zh, y = place()
     cap, chans, feat = es_ref.shape[1], 128, x_in.shape[1]
@@ -163,7 +166,8 @@
     up, down = (y + 1) % 4, (y + 3) % 4
     zs = [(pair(zl, d) if d else zl, (1 - zh) if far_z else zh) for far_z in (0, 1) for d in range(4)][1:]
     ags = [((rep + dr) % 2, (y + dy) % 4) for dr in (0, 1) for dy in range(4)][1:]
-    lines = [pair(zl, d) for d in (1, 2, 3)]
+    inner = ((zl + 1) // 2) % 2 == 1
+    mate, inward, beyond = pair(zl, 1), 2 - zl // 2, 3 - 3 * (zl // 2)
     across, other = device(rep, zl, x, 1 - zh, y), device(1 - rep, zl, x, zh, y)
 
     def on_x(nx):
@@ -198,27 +202,55 @@
         ref = out_ref.at[slots[1], 8:, at]
         return a, far.start(ref, ref, to(two))
 
-    z_go = [None, None]
     xs, ends_g, ends_x, ys = ([], []), ([], []), [], []
-
-    def z_start(p):
-        at = parts[p]
-        z_go[p] = [far.start(g_in.at[:, at], g_ref.at[mine_g, :, at], on_z(n)) for n in lines]
-
-    z_start(0)
-    hop = far.start(x_in, x_ref.at[mine_x], across)
+    order = [zl, mate, inward, beyond]
+
+    def hand(p, who, sent, got, to):
+        dst = g_ref.at[who * 4 + x, :, parts[p]]
+        return pltpu.make_async_remote_copy(
+            src_ref=g_in.at[:, parts[p]] if who is zl else dst, dst_ref=dst,
+            send_sem=line_send.at[5 * p + sent], recv_sem=line_recv.at[3 * p + got],
+            device_id=on_z(to), device_id_type=MESH,
+        )
+
+    def line_start(p):
+        hand(p, zl, 0, 0, mate).start()
+
+        @pl.when(inner)
+        def _():
+            hand(p, zl, 1, 1, inward).start()
+
+    def line_next(p, k):
+        hand(p, order[k + 1], 0, k, mate).wait_recv()
+
+        @pl.when(inner)
+        def _():
+            if k == 0:
+                hand(p, mate, 2, 2, inward).start()
+            elif k == 1:
+                hand(p, inward, 3, 1, mate).start()
+            else:
+                hand(p, beyond, 4, 2, mate).start()
+
+    def line_drain(p):
+        hand(p, zl, 0, 0, mate).wait_send()
+
+        @pl.when(inner)
+        def _():
+            for k in range(1, 5):
+                hand(p, zl, k, 0, mate).wait_send()
+
+    line_start(0)
     xs[0].append(both(g_in.at[:, parts[0]], mine_g, parts[0], g_ref, on_x, right, left))
     ys.append(both(x_in, mine_x, whole, x_ref, on_y, up, down))
-    z_start(1)
     xs[1].append(both(g_in.at[:, parts[1]], mine_g, parts[1], g_ref, on_x, right, left))
     owned.append(pltpu.make_async_copy(g_in, g_ref.at[mine_g], own.at[6]))
     owned.append(pltpu.make_async_copy(x_in, x_ref.at[mine_x], own.at[7]))
     for copy in owned:
         copy.start()
-    order = [zl, *lines]
 
     def x_step(p, j):
-        z_go[p][j - 1].wait_recv()
+        line_next(p, j - 1)
         slot = order[j] * 4 + x
         xs[p].append(both(g_ref.at[slot, :, parts[p]], slot, parts[p], g_ref, on_x, right, left))
 
@@ -250,22 +282,23 @@
         lax.fori_loop(0, src.shape[0] // 128, cut, 0)
 
     x_step(0, 1)
+    hop = far.start(x_in, x_ref.at[mine_x], across)
     x_relay(0, 0)
+    x_step(0, 2)
+    line_start(1)
+    x_relay(0, 1)
     y_relay(0)
-    x_step(0, 2)
-    x_relay(0, 1)
+    x_step(0, 3)
+    x_relay(0, 2)
     hop.wait_recv()
     slot = (1 - zh) * 4 + y
     ys.append(both(x_ref.at[slot], slot, whole, x_ref, on_y, up, down))
-    x_step(0, 3)
-    x_relay(0, 2)
-    y_relay(1)
     x_step(1, 1)
     x_relay(0, 3)
     x_relay(1, 0)
     x_step(1, 2)
-    for copy in ends_x:
-        copy.wait_recv()
+    y_relay(1)
+    x_relay(1, 1)
 
     zrefs = (z0_ref, z1_ref, z2_ref)
 
@@ -276,12 +309,13 @@
         zrefs[order][0, rows, at] = hi
         zrefs[order][1, rows, at] = lo
 
+    x_step(1, 3)
+    for copy in ends_x:
+        copy.wait_recv()
     pick(x_ref, hs_ref, rows_ref, 0, 5 * chans, 5)
-    x_relay(1, 1)
-    x_step(1, 3)
     x_relay(1, 2)
+    x_relay(1, 3)
     rotate(rows_ref, rot_ref, put_z, chans, cap, range(5))
-    x_relay(1, 3)
 
     urefs = (u0_ref, u1_ref, u2_ref)
     vrefs = (None, v1_ref, v2_ref)
@@ -327,11 +361,11 @@
                             s * per + done : s * per + done + n, j * chans : (j + 1) * chans
                         ]
             base += cols * per
-        for blk, off, done, n in pieces(base, 8 * quarter - base, quarter):
+        for blk, off, done, n in pieces(base, PACK - base, quarter):
             wg[2 * h : 2 * h + 2, :, blk, off : off + n, :] = jnp.zeros((2, 4, n, chans), F32)
         for nx in xorder:
             zz = pl.ds(2 * h, 2)
-            swaps.append(far.start(wg.at[zz, nx, pl.ds(4 * (1 - rep), 4)], halves.at[zz, nx], other))
+            swaps.append(far.start(wg.at[zz, nx, pl.ds(8 * (1 - rep), 8)], halves.at[zz, nx], other))
 
     def three(w, u):
         return mm(w[0], u[0], NN) + mm(w[0], u[1], NN) + mm(w[1], u[0], NN)
@@ -348,28 +382,46 @@
         swaps[i].wait_recv()
         swaps[4 + i].wait_recv()
         nx = xorder[i]
-        halves[:, nx] = wg[:, nx, pl.ds(4 * rep, 4)] + halves[:, nx]
-
-    def x_part(nx, h):
+        halves[:, nx] = wg[:, nx, pl.ds(8 * rep, 8)] + halves[:, nx]
+
+    def ring_sum(dst, part, me, copies, ins):
+        for copy in copies:
+            copy.wait_recv()
+        for h in range(2):
+            dst(h)[...] = part(me, h)[...] + ins[0, h] + ins[1, h]
+
+    def a_part(nx, h):
         return halves.at[:, nx, pl.ds(2 * h, 2)]
+
+    def b_part(ny, h):
+        return halves.at[pl.ds(2 * h, 2), :, 4 + ny]
+
+    def a2_part(ny, h):
+        return wa.at[pl.ds(2 * h, 2), ny]
+
+    def b2_part(nx, h):
+        return wb.at[pl.ds(2 * h, 2), nx]
 
     keep(0, three(wh0, u0_ref))
     keep(2, three(wh2r, u2_ref) + three(wh2i, v2_ref))
     fold(0)
-    x_first = ring_first(far, x, x_part, x_hops, on_x)
+    a_first = ring_first(far, x, a_part, a_hops, on_x)
     fold(1)
     fold(2)
-    x_rest = ring_own(far, x, x_part, x_ins, on_x)
+    a_rest = ring_own(far, x, a_part, a_ins, on_x)
     fold(3)
+    b_first = ring_first(far, y, b_part, b_hops, on_y)
+    b_rest = ring_own(far, y, b_part, b_ins, on_y)
     keep(1, three(wh1r, u1_ref) + three(wh1i, v1_ref))
-    x_rest += ring_rest(far, x, x_part, x_first, x_hops, x_ins, on_x)
+    a_rest += ring_rest(far, x, a_part, a_first, a_hops, a_ins, on_x)
+    b_rest += ring_rest(far, y, b_part, b_first, b_hops, b_ins, on_y)
 
     tiles = cap // 128
 
-    def back(i, carry):
+    def back(levels, i, carry):
         ch = pl.multiple_of((i // tiles) * 16, 16)
         ln = pl.multiple_of((i % tiles) * 128, 128)
-        for level in range(5):
+        for level in levels:
             q, cols = min(level, 2), 2 * level + 1
             ds = []
             for r in range(2 * q + 1):
@@ -388,60 +440,67 @@
                 term_ref[rows, pl.ds(ln + cap, 128)] = lo
         return carry
 
-    lax.fori_loop(0, (chans // 16) * tiles, back, 0)
-
-    def scatter(c, carry):
-        at = pl.multiple_of(c * 5 * chans, chans)
-        res = mm(hs2_ref[...], term_ref[pl.ds(at, 5 * chans), :], NT)
-        total[:, :, :, pl.ds(at, 5 * chans)] = res.reshape(2, 4, 16, 5 * chans)
-        return carry
-
-    lax.fori_loop(0, 5, scatter, 0)
-
-    def f_part(ny, h):
-        return total.at[:, ny, pl.ds(8 * h, 8)]
-
-    f_first = ring_first(far, y, f_part, f_hops, on_y)
-    f_rest = ring_own(far, y, f_part, f_ins, on_y)
-    for copy in x_rest:
-        copy.wait_recv()
-    for h in range(2):
-        at = pl.ds(2 * h, 2)
-        w1[:, at] = halves[:, x, at] + x_ins[0, h] + x_ins[1, h]
-
-    def y_part(ny, h):
-        return w1.at[:, ny, pl.ds(40 * h, 40)]
-
-    y_first = ring_first(far, y, y_part, y_hops, on_y)
-    f_rest += ring_rest(far, y, f_part, f_first, f_hops, f_ins, on_y)
-    y_rest = ring_own(far, y, y_part, y_ins, on_y)
-    y_rest += ring_rest(far, y, y_part, y_first, y_hops, y_ins, on_y)
-    for copy in f_rest:
-        copy.wait_recv()
-    for h in range(2):
-        at = pl.ds(8 * h, 8)
-        f_mine[:, at] = total[:, y, at] + f_ins[0, h] + f_ins[1, h]
-    f_swap = far.start(f_mine.at[1 - zh], f_got, across)
-    for copy in y_rest:
-        copy.wait_recv()
-    for h in range(2):
-        at = pl.ds(40 * h, 40)
-        w2[:, at] = w1[:, y, at] + y_ins[0, h] + y_ins[1, h]
+    def f_view(ref, p):
+        return ref.at[..., parts[p]]
+
+    def f_part(p):
+        return lambda ny, h: total.at[:, ny, pl.ds(8 * h, 8), parts[p]]
+
+    f_first, f_rest = [], []
+    for p, (levels, first, width, count) in enumerate(
+        ((range(4), 0, 4 * chans, 4), ((4,), 16 * chans, 3 * chans, 3))
+    ):
+        lax.fori_loop(0, (chans // 16) * tiles, functools.partial(back, levels), 0)
+
+        def scatter(c, carry, first=first, width=width):
+            at = pl.multiple_of(first + c * width, 128)
+            res = mm(hs2_ref[...], term_ref[pl.ds(at, width), :], NT)
+            total[:, :, :, pl.ds(at, width)] = res.reshape(2, 4, 16, width)
+            return carry
+
+        lax.fori_loop(0, count, scatter, 0)
+        f_first.append(ring_first(far, y, f_part(p), f_view(f_hops, p), on_y))
+        f_rest.append(ring_own(far, y, f_part(p), f_view(f_ins, p), on_y))
+
+    def f_on(p):
+        f_rest[p] += ring_rest(far, y, f_part(p), f_first[p], f_view(f_hops, p), f_view(f_ins, p), on_y)
+
+    def f_across(p):
+        ring_sum(
+            lambda h: f_mine.at[:, pl.ds(8 * h, 8), parts[p]], f_part(p), y, f_rest[p], f_view(f_ins, p)
+        )
+        return far.start(f_mine.at[1 - zh, :, parts[p]], f_got.at[:, parts[p]], across)
+
+    ring_sum(lambda h: wa.at[:, pl.ds(2 * h, 2)], a_part, x, a_rest, a_ins)
+    a2_first = ring_first(far, y, a2_part, a2_hops, on_y)
+    a2_rest = ring_own(far, y, a2_part, a2_ins, on_y)
+    ring_sum(lambda h: wb.at[pl.ds(2 * h, 2)], b_part, y, b_rest, b_ins)
+    b2_first = ring_first(far, x, b2_part, b2_hops, on_x)
+    b2_rest = ring_own(far, x, b2_part, b2_ins, on_x)
+    f_on(0)
+    a2_rest += ring_rest(far, y, a2_part, a2_first, a2_hops, a2_ins, on_y)
+    b2_rest += ring_rest(far, x, b2_part, b2_first, b2_hops, b2_ins, on_x)
+    f_on(1)
+    f_swap = [f_across(0)]
+    ring_sum(lambda h: w2.at[pl.ds(2 * h, 2), 0], a2_part, y, a2_rest, a2_ins)
+    ring_sum(lambda h: w2.at[pl.ds(2 * h, 2), 1], b2_part, x, b2_rest, b2_ins)
     z_made = [far.start(w2.at[a], z_got.at[i], device(rep, a, x, b, y)) for i, (a, b) in enumerate(zs)]
+    f_swap.append(f_across(1))
     w3 = w2[zl]
     for i, copy in enumerate(z_made):
         copy.wait_recv()
         w3 = w3 + z_got[i]
-    slot = rep * 4 + y
-    packed[slot] = w3
-    ag_made = [
-        far.start(packed.at[slot], packed.at[slot], device(a, zl, x, zh, b)) for a, b in ags
-    ]
-    f_swap.wait_recv()
+    packed[rep, :, y] = w3
+    mine = packed.at[rep, :, y]
+    ag_made = [far.start(mine, mine, device(a, zl, x, zh, b)) for a, b in ags]
+    for copy in f_swap:
+        copy.wait_recv()
     out[...] = f_mine[zh] + f_got[...]
     for copy in ag_made:
         copy.wait_recv()
     far.drain()
+    line_drain(0)
+    line_drain(1)
 
 
 def finish_kernel(feats, packed, out, o0, o1, o2, o3, o4):
@@ -460,16 +519,16 @@
     chans = 128
     rows, feat = src_feats.shape
     src_blk, tgt_blk = n_tgt * rows, owners * rows
-    q = PACK // 8
+    q = PACK // 16
     vm = pl.BlockSpec(memory_space=pltpu.VMEM)
     anywhere = pl.BlockSpec(memory_space=pl.ANY)
     dims = [w.shape[0] for w in weights]
-    count = 2 * 19 + 9 + 8 + 6 + 6 + 1 + 6 + 7 + 7
+    count = 2 * 16 + 9 + 8 + 4 * 6 + 2 * 7 + 7 + 7
     feats, packed = pl.pallas_call(
         tile_kernel,
         out_shape=(
             jax.ShapeDtypeStruct((rows, feat), F32),
-            jax.ShapeDtypeStruct((8, q, chans), F32),
+            jax.ShapeDtypeStruct((2, 2, 4, q, chans), F32),
         ),
         in_specs=[pl.BlockSpec(memory_space=pltpu.SMEM), vm, vm] + [anywhere] * 8,
         out_specs=(vm, vm),
@@ -493,21 +552,28 @@
             pltpu.VMEM((2, dims[3], 2 * cap), BF16),
             pltpu.VMEM((feat, 2 * cap), BF16),
             pltpu.VMEM((2, 4, rows, feat), F32),
-            pltpu.VMEM((4, 4, 8, q, chans), F32),
+            pltpu.VMEM((4, 4, 16, q, chans), F32),
             pltpu.VMEM((2, 2, 8, feat), F32),
             pltpu.VMEM((2, 2, 2, 8, feat), F32),
             pltpu.VMEM((2, rows, feat), F32),
             pltpu.VMEM((rows, feat), F32),
-            pltpu.VMEM((4, 4, 4, q, chans), F32),
+            pltpu.VMEM((4, 4, 8, q, chans), F32),
             pltpu.VMEM((2, 4, 2, q, chans), F32),
             pltpu.VMEM((2, 2, 4, 2, q, chans), F32),
+            pltpu.VMEM((2, 2, 4, q, chans), F32),
+            pltpu.VMEM((2, 2, 2, 4, q, chans), F32),
             pltpu.VMEM((4, 4, q, chans), F32),
-            pltpu.VMEM((2, 4, q // 2, chans), F32),
-            pltpu.VMEM((2, 2, 4, q // 2, chans), F32),
-            pltpu.VMEM((4, q, chans), F32),
-            pltpu.VMEM((7, q, chans), F32),
+            pltpu.VMEM((4, 4, q, chans), F32),
+            pltpu.VMEM((2, 2, q, chans), F32),
+            pltpu.VMEM((2, 2, 2, q, chans), F32),
+            pltpu.VMEM((2, 2, q, chans), F32),
+            pltpu.VMEM((2, 2, 2, q, chans), F32),
+            pltpu.VMEM((4, 2, q, chans), F32),
+            pltpu.VMEM((7, 2, q, chans), F32),
             pltpu.SemaphoreType.DMA((count,)),
             pltpu.SemaphoreType.DMA((count,)),
+            pltpu.SemaphoreType.DMA((10,)),
+            pltpu.SemaphoreType.DMA((6,)),
             pltpu.SemaphoreType.DMA((8,)),
         ],
         compiler_params=pltpu.CompilerParams(
@@ -524,7 +590,7 @@
         in_specs=[vm, vm],
         out_specs=(vm,) * 6,
         name="finish",
-    )(feats, packed)
+    )(feats, packed.reshape(16, q, chans))
 
 
 def local(src_feats, tgt_cotangent, rotation, edge_src, edge_tgt, edge_count, *weights):

time: 125 us -> 118 us (0.944)
  Pallas kernels: 123 us -> 117 us
    pallas_call x1, Pallas kernels: 121 us -> 115 us  [run(): pl.pallas_call(tile_kernel, out_shape=(jax.ShapeDtypeStruct((rows, feat),...]
where the time goes in v4:
time: 118 us
  Pallas kernels  117 us (99%)
  between operations  1.29 us (1%)
    pallas_call x1, Pallas kernels, run(): pl.pallas_call(tile_kernel, out_shape=(jax.ShapeDtypeStruct((rows, feat),...  115 us

profile of v4, /device:TPU:1, one launch (start us, length us, event | category | flops | bytes accessed | tf_op | source)
XLA Modules:
  0.0 118.1 jit_solution(10485948806149699239)
XLA Ops:
  1.3 114.9 %tile.1 = (f32[16,3200]{1,0:T(8,128)}, f32[2,2,4,40,128]{4,3,2,1,0:T(8,128)}) custom-call(s32[1]{0:T(128)} %bitcast.8.cnt_ref, s32[1,384]{1,0:T(1,128)} %bitcast.13, s32[1,384]{1,0:T(1,128)} %bitcast.14, f32[16,3200]{1,0:T(8,128)} %bitcast.10, f32[16,3200]{1,0:T(8,128)} %bitcast.11, f32[115,1,384]{2,1,0:T(1,128)} %bitcast.12, f32[640,640]{1,0:T(8,128)} %w0_in.1, ...), custom_call_target="tpu_custom_call" | custom-call | tf_op jit(solution)/shard_map/tile/pallas_call | solution.py:527
  116.2 1.9 %finish.1 = (f32[16,3200]{1,0:T(8,128)}, f32[40,640]{1,0:T(8,128)}, f32[32,512]{1,0:T(8,128)}, f32[32,512]{1,0:T(8,128)}, f32[24,384]{1,0:T(8,128)}, /*index=5*/f32[24,384]{1,0:T(8,128)}) custom-call(f32[16,3200]{1,0:T(8,128)} %get-tuple-element.14.feats, f32[16,40,128]{2,1,0:T(8,128)} %bitcast.9), custom_call_target="tpu_custom_call" | custom-call | tf_op jit(solution)/shard_map/finish/pallas_call | solution.py:584

commit v5 on v4

--- a/solution.py
+++ b/solution.py
@@ -164,9 +164,10 @@
 
     right, left = (x + 1) % 4, (x + 3) % 4
     up, down = (y + 1) % 4, (y + 3) % 4
-    zs = [(pair(zl, d) if d else zl, (1 - zh) if far_z else zh) for far_z in (0, 1) for d in range(4)][1:]
+    zs = [(pair(zl, d), zh) for d in (1, 2, 3)] + [(zl, 1 - zh)]
     ags = [((rep + dr) % 2, (y + dy) % 4) for dr in (0, 1) for dy in range(4)][1:]
     inner = ((zl + 1) // 2) % 2 == 1
+    pair_rest = (pair(zl, 2), pair(zl, 3))
     mate, inward, beyond = pair(zl, 1), 2 - zl // 2, 3 - 3 * (zl // 2)
     across, other = device(rep, zl, x, 1 - zh, y), device(1 - rep, zl, x, zh, y)
 
@@ -342,7 +343,7 @@
 
     def grad(z, u, at, count):
         zhi, zlo = z[0, pl.ds(at, count), :], z[1, pl.ds(at, count), :]
-        return mm(zhi, u[0], NT) + mm(zhi, u[1], NT) + mm(zlo, u[0], NT)
+        return mm(jnp.concatenate([zhi, zhi, zlo], 1), jnp.concatenate([u[0], u[1], u[0]], 1), NT)
 
     quarter = wg.shape[3]
     xorder = [(x + 2) % 4, right, left, x]
@@ -368,7 +369,7 @@
             swaps.append(far.start(wg.at[zz, nx, pl.ds(8 * (1 - rep), 8)], halves.at[zz, nx], other))
 
     def three(w, u):
-        return mm(w[0], u[0], NN) + mm(w[0], u[1], NN) + mm(w[1], u[0], NN)
+        return mm(jnp.concatenate([w[0], w[0], w[1]], 1), jnp.concatenate([u[0], u[1], u[0]], 0), NN)
 
     firsts = (0, 5 * chans, 13 * chans)
 
@@ -454,7 +455,7 @@
 
         def scatter(c, carry, first=first, width=width):
             at = pl.multiple_of(first + c * width, 128)
-            res = mm(hs2_ref[...], term_ref[pl.ds(at, width), :], NT)
+            res = mm(term_ref[pl.ds(at, width), :], hs2_ref[...], NT).T
             total[:, :, :, pl.ds(at, width)] = res.reshape(2, 4, 16, width)
             return carry
 
@@ -484,12 +485,16 @@
     f_swap = [f_across(0)]
     ring_sum(lambda h: w2.at[pl.ds(2 * h, 2), 0], a2_part, y, a2_rest, a2_ins)
     ring_sum(lambda h: w2.at[pl.ds(2 * h, 2), 1], b2_part, x, b2_rest, b2_ins)
-    z_made = [far.start(w2.at[a], z_got.at[i], device(rep, a, x, b, y)) for i, (a, b) in enumerate(zs)]
+    z_made = [far.start(w2.at[a], z_got.at[i], on_z(a)) for i, a in enumerate((mate, *pair_rest))]
     f_swap.append(f_across(1))
     w3 = w2[zl]
     for i, copy in enumerate(z_made):
         copy.wait_recv()
         w3 = w3 + z_got[i]
+    z_got[3] = w3
+    swap = far.start(z_got.at[3], z_got.at[4], across)
+    swap.wait_recv()
+    w3 = w3 + z_got[4]
     packed[rep, :, y] = w3
     mine = packed.at[rep, :, y]
     ag_made = [far.start(mine, mine, device(a, zl, x, zh, b)) for a, b in ags]
@@ -569,7 +574,7 @@
             pltpu.VMEM((2, 2, q, chans), F32),
             pltpu.VMEM((2, 2, 2, q, chans), F32),
             pltpu.VMEM((4, 2, q, chans), F32),
-            pltpu.VMEM((7, 2, q, chans), F32),
+            pltpu.VMEM((5, 2, q, chans), F32),
             pltpu.SemaphoreType.DMA((count,)),
             pltpu.SemaphoreType.DMA((count,)),
             pltpu.SemaphoreType.DMA((10,)),

time: 118 us -> 118 us (level)
  no operation moved by 1% of the time
where the time goes in v5:
time: 118 us
  Pallas kernels  117 us (99%)
  between operations  1.29 us (1%)
    pallas_call x1, Pallas kernels, run(): pl.pallas_call(tile_kernel, out_shape=(jax.ShapeDtypeStruct((rows, feat),...  115 us

profile of v5, /device:TPU:1, one launch (start us, length us, event | category | flops | bytes accessed | tf_op | source)
XLA Modules:
  0.0 117.8 jit_solution(14030021640544895444)
XLA Ops:
  1.3 114.7 %tile.1 = (f32[16,3200]{1,0:T(8,128)}, f32[2,2,4,40,128]{4,3,2,1,0:T(8,128)}) custom-call(s32[1]{0:T(128)} %bitcast.8.cnt_ref, s32[1,384]{1,0:T(1,128)} %bitcast.13, s32[1,384]{1,0:T(1,128)} %bitcast.14, f32[16,3200]{1,0:T(8,128)} %bitcast.10, f32[16,3200]{1,0:T(8,128)} %bitcast.11, f32[115,1,384]{2,1,0:T(1,128)} %bitcast.12, f32[640,640]{1,0:T(8,128)} %w0_in.1, ...), custom_call_target="tpu_custom_call" | custom-call | tf_op jit(solution)/shard_map/tile/pallas_call | solution.py:532
  116.0 1.9 %finish.1 = (f32[16,3200]{1,0:T(8,128)}, f32[40,640]{1,0:T(8,128)}, f32[32,512]{1,0:T(8,128)}, f32[32,512]{1,0:T(8,128)}, f32[24,384]{1,0:T(8,128)}, /*index=5*/f32[24,384]{1,0:T(8,128)}) custom-call(f32[16,3200]{1,0:T(8,128)} %get-tuple-element.14.feats, f32[16,40,128]{2,1,0:T(8,128)} %bitcast.9), custom_call_target="tpu_custom_call" | custom-call | tf_op jit(solution)/shard_map/finish/pallas_call | solution.py:589
